TPU v7x, 1024 devices: a whole 4x8x16 slice. The times are simulated.
1024 devices in a mesh: expert: 64 (over y_lo, z, core), hidden: 16 (over x, y_hi).
Axes of the slice: x: 4, y: 8 (y_hi: 4, y_lo: 2; y = y_hi * 2 + y_lo), z: 16, core: 2. Of those that a mesh axis runs over, the one named last changes fastest.
Arguments:
- tokens: bfloat16 [1024, 2048], P('expert', 'hidden'), may hold values from -6 to 6
- out_cotangent: bfloat16 [1024, 2048], P('expert', 'hidden'), may hold values from -24 to 24
- expert_ids: int32 [1024, 8], P('expert'), may hold values from 0 to 63, all different within a row; in each aligned block of 16 rows (0 to 15, 16 to 31, ...) at most 4 rows name the same one
- gate_probs: float32 [1024, 8], P('expert'), may hold values from 0.05 to 0.35
- relocate: int32 [64], replicated, may hold values from 0 to 1, as said below
- w_gate: bfloat16 [64, 2048, 1536], P('expert', None, 'hidden'), may hold values from -0.125 to 0.125
- w_up: bfloat16 [64, 2048, 1536], P('expert', None, 'hidden'), may hold values from -0.125 to 0.125
- w_down: bfloat16 [64, 1536, 2048], P('expert', 'hidden'), may hold values from -0.15625 to 0.15625
- moment_gate: bfloat16 [64, 2048, 1536], P('expert', None, 'hidden'), may hold values from -3 to 3
- moment_up: bfloat16 [64, 2048, 1536], P('expert', None, 'hidden'), may hold values from -3 to 3
- moment_down: bfloat16 [64, 1536, 2048], P('expert', 'hidden'), may hold values from -3 to 3
Outputs:
- token_grad: bfloat16 [1024, 2048], P('expert', 'hidden')
- new_moment_gate: bfloat16 [64, 2048, 1536], P('expert', None, 'hidden')
- new_moment_up: bfloat16 [64, 2048, 1536], P('expert', None, 'hidden')
- new_moment_down: bfloat16 [64, 1536, 2048], P('expert', 'hidden')
Inputs may be any that keep to these rules, and one draw needn't show every extreme that they name: `expert_ids`: in each group of 16 consecutive tokens no expert is named more than 4 times, a bound that some block reaches. relocate[s] equals relocate[(s + 32) mod 64]; exactly half of these pairs of slots have 1.
All inputs are finite; a program needn't handle non-finite values.
Results may differ from a plain program's by a relative error of at most 0.015.
Values may be sent and summed in bfloat16 or wider, within the bound.
A program may use at most 128 MiB of HBM per device.

v0:
```python
import jax
import jax.numpy as jnp
from jax import lax
from jax.sharding import PartitionSpec as P

MOMENT_DECAY = 0.9
ROW_DIMS = (((0,), (0,)), ((), ()))
UNIT_DIMS = (((1,), (1,)), ((), ()))


def partner_2(block, axis, bit):
    count = lax.axis_size(axis)
    route = []
    for low in range(count):
        high = low | 1 << bit
        if high != low and high < count:
            route += [(low, high), (high, low)]
    return lax.ppermute(block, axis, route)


def routing_matrices(expert_ids, gate_probs, destination, capacity, expert_count):
    tok_rows, top_count = expert_ids.shape
    flat_ids = expert_ids.reshape(tok_rows * top_count)
    experts_iota = jnp.arange(expert_count, dtype=jnp.int32)
    onehot = (flat_ids[:, None] == experts_iota[None, :]).astype(jnp.int32)
    ranks = jnp.sum((jnp.cumsum(onehot, axis=0) - onehot) * onehot, axis=1)
    targets = jnp.sum(onehot * destination[None, :], axis=1)
    slots = (targets * capacity + ranks).reshape(tok_rows, top_count)
    slot_iota = jnp.arange(expert_count * capacity, dtype=jnp.int32)
    matches = slots[None, :, :] == slot_iota[:, None, None]
    placement = jnp.any(matches, axis=2).astype(jnp.float32)
    weighted = jnp.sum(jnp.where(matches, gate_probs[None, :, :], 0.0), axis=2)
    return (placement, weighted)


def update_moment(moment, gradient):
    return (MOMENT_DECAY * moment.astype(jnp.float32) + (1.0 - MOMENT_DECAY) * gradient).astype(
        jnp.bfloat16
    )


def on_device(
    tokens,
    out_cotangent,
    expert_ids,
    gate_probs,
    relocate,
    w_gate,
    w_up,
    w_down,
    moment_gate,
    moment_up,
    moment_down,
):
    expert_count = lax.axis_size("expert")
    tok_rows, top_count = expert_ids.shape
    capacity = min(tok_rows, 2 * tok_rows * top_count // expert_count)
    half = expert_count // 2
    pair_bit = expert_count.bit_length() - 2
    experts_iota = jnp.arange(expert_count, dtype=jnp.int32)
    my_slot = lax.axis_index("expert")
    swapping = jnp.sum(jnp.where(experts_iota == my_slot, relocate, 0)) == 1
    partner = (experts_iota + half) % expert_count
    arrived = partner_2(
        (w_gate[0], w_up[0], w_down[0], moment_gate[0], moment_up[0], moment_down[0]),
        "expert",
        pair_bit,
    )
    resident = (w_gate[0], w_up[0], w_down[0], moment_gate[0], moment_up[0], moment_down[0])
    chosen = [jnp.where(swapping, incoming, kept) for incoming, kept in zip(arrived, resident)]
    gate_now, up_now, down_now = (chosen[0], chosen[1], chosen[2])
    moments_now = (chosen[3], chosen[4], chosen[5])
    destination = jnp.where(relocate == 1, partner, experts_iota)
    placement, weighted = routing_matrices(
        expert_ids, gate_probs, destination, capacity, expert_count
    )
    rows_count = expert_count * capacity
    slice_width = tokens.shape[1]
    model_width = gate_now.shape[0]
    x_send = jnp.dot(
        placement.astype(jnp.bfloat16), tokens, preferred_element_type=jnp.float32
    ).astype(jnp.bfloat16)
    dy_send = jnp.dot(
        weighted, out_cotangent.astype(jnp.float32), precision=lax.Precision.HIGHEST
    ).astype(jnp.bfloat16)
    x_recv, dy_recv = (
        lax.all_to_all(
            x_send.reshape(expert_count, capacity, slice_width),
            "expert",
            split_axis=0,
            concat_axis=0,
            tiled=True,
        ),
        lax.all_to_all(
            dy_send.reshape(expert_count, capacity, slice_width),
            "expert",
            split_axis=0,
            concat_axis=0,
            tiled=True,
        ),
    )
    x_recv = x_recv.reshape(rows_count, slice_width)
    dy_recv = dy_recv.reshape(rows_count, slice_width)
    x_full, dy_full = (
        lax.all_gather(x_recv, "hidden", axis=1, tiled=True),
        lax.all_gather(dy_recv, "hidden", axis=1, tiled=True),
    )
    gate_pre = jnp.dot(x_full, gate_now, preferred_element_type=jnp.float32)
    up_pre = jnp.dot(x_full, up_now, preferred_element_type=jnp.float32)
    back = lax.dot_general(dy_full, down_now, UNIT_DIMS, preferred_element_type=jnp.float32)
    sig = jax.nn.sigmoid(gate_pre)
    act = gate_pre * sig
    hidden = (act * up_pre).astype(jnp.bfloat16)
    d_gate = (back * up_pre * sig * (1.0 + gate_pre * (1.0 - sig))).astype(jnp.bfloat16)
    d_up = (back * act).astype(jnp.bfloat16)
    grad_gate = lax.dot_general(x_full, d_gate, ROW_DIMS, preferred_element_type=jnp.float32)
    grad_up = lax.dot_general(x_full, d_up, ROW_DIMS, preferred_element_type=jnp.float32)
    grad_down = lax.dot_general(hidden, dy_full, ROW_DIMS, preferred_element_type=jnp.float32)
    partial_value = lax.dot_general(d_gate, gate_now, UNIT_DIMS, preferred_element_type=jnp.float32)
    partial_value = partial_value + lax.dot_general(
        d_up, up_now, UNIT_DIMS, preferred_element_type=jnp.float32
    )
    fresh_gate = update_moment(moments_now[0], grad_gate)
    fresh_up = update_moment(moments_now[1], grad_up)
    fresh_down = update_moment(moments_now[2], grad_down)
    summed = lax.psum_scatter(
        partial_value.reshape(expert_count, capacity, model_width).astype(jnp.bfloat16),
        "hidden",
        scatter_dimension=2,
        tiled=True,
    ).astype(jnp.float32)
    returned = lax.all_to_all(
        summed.astype(jnp.bfloat16), "expert", split_axis=0, concat_axis=0, tiled=True
    ).astype(summed.dtype)
    token_sum = jnp.dot(
        placement.T,
        returned.reshape(rows_count, slice_width),
        precision=lax.Precision.HIGHEST,
        preferred_element_type=jnp.float32,
    )
    token_grad = token_sum.astype(jnp.bfloat16)
    return (token_grad, fresh_gate[None], fresh_up[None], fresh_down[None])


def solution(mesh):
    return jax.shard_map(
        on_device,
        mesh=mesh,
        in_specs=(
            P("expert", "hidden"),
            P("expert", "hidden"),
            P("expert", None),
            P("expert", None),
            P(),
            P("expert", None, "hidden"),
            P("expert", None, "hidden"),
            P("expert", "hidden", None),
            P("expert", None, "hidden"),
            P("expert", None, "hidden"),
            P("expert", "hidden", None),
        ),
        out_specs=(
            P("expert", "hidden"),
            P("expert", None, "hidden"),
            P("expert", None, "hidden"),
            P("expert", "hidden", None),
        ),
        check_vma=False,
    )
```

profile of v0, /device:TPU:1, one launch (start us, length us, event | category | flops | bytes accessed | tf_op | source)
XLA Modules:
  0.0 447.2 jit_solution(7793152509020359865)
XLA Ops:
  7.2 0.8 copy.21
  8.2 1.3 fusion.14
  10.3 36.3 %all_to_all.15 = bf16[64,4,128]{2,1,0:T(4,128)(2,1)} all-to-all(bf16[64,4,128]{2,1,0:T(4,128)(2,1)S(1)} %bitcast.69), channel_id=1, replica_groups=mesh['expert'=64,'hidden'=16] {'expert'}, dimensions={0} | all-to-all | bytes 131072 | tf_op jit(solution)/shard_map/all_to_all | solution.py:87
  46.7 0.8 copy.22
  47.6 1.0 convolution_convert_fusion.1
  48.6 19.0 %all_to_all.16 = bf16[64,4,128]{2,1,0:T(4,128)(2,1)} all-to-all(bf16[64,4,128]{2,1,0:T(4,128)(2,1)S(1)} %bitcast.68), channel_id=1, replica_groups=mesh['expert'=64,'hidden'=16] {'expert'}, dimensions={0} | all-to-all | bytes 131072 | tf_op jit(solution)/shard_map/all_to_all | solution.py:94
  67.6 2.0 collective-permute-start.1
  69.7 3.2 collective-permute-start.2
  72.9 2.0 collective-permute-start
  75.6 4.4 collective-permute-done.1
  80.0 29.9 %all-gather.5.cloned.1.call-done = bf16[256,2048]{1,0:T(8,128)(2,1)} async-done(((bf16[256,128]{1,0:T(8,128)(2,1)}), bf16[256,2048]{1,0:T(8,128)(2,1)}) %all-gather.5.cloned.1.call-update) | async-done | bytes 1048592 | tf_op jit(solution)/shard_map/all_gather | solution.py:105
  110.0 1.8 fusion.8
  111.8 1.8 fusion.9
  113.6 65.2 %all-gather.3.cloned.1.call-done = bf16[256,2048]{1,0:T(8,128)(2,1)} async-done(((bf16[256,128]{1,0:T(8,128)(2,1)}), bf16[256,2048]{1,0:T(8,128)(2,1)}) %all-gather.3.cloned.1.call-update) | async-done | bytes 1048592 | tf_op jit(solution)/shard_map/all_gather | solution.py:106
  178.8 1.7 multiply_convert_fusion.2
  180.6 0.5 fusion.7
  181.2 0.5 fusion
  182.0 52.8 %copy.23 = bf16[64,4,2048]{1,0,2:T(8,128)(2,1)} copy(bf16[64,4,2048]{2,1,0:T(4,128)(2,1)S(1)} %convert_element_type.63) | data formatting | bytes 2097152
  234.9 63.6 %reshape.46 = bf16[2048,256]{1,0:T(8,128)(2,1)} reshape(bf16[2048,64,4]{2,1,0:T(8,128)(2,1)} %bitcast.59) | data formatting | bytes 2097152
  298.5 2.9 collective-permute-start.3
  301.4 2.4 collective-permute-start.4
  303.8 2.9 collective-permute-start.5
  306.7 1.7 collective-permute-done.3
  308.4 1.1 fusion.1
  309.6 91.3 %reduce-scatter.4.cloned.1.call-done = bf16[128,256]{1,0:T(8,128)(2,1)} async-done(((bf16[2048,256]{1,0:T(8,128)(2,1)}), bf16[128,256]{1,0:T(8,128)(2,1)}) %reduce-scatter.4.cloned.1.call-update) | async-done | bytes 65552
  400.9 5.3 %reshape.47 = bf16[128,64,4]{2,1,0:T(8,128)(2,1)S(1)} reshape(bf16[128,256]{1,0:T(8,128)(2,1)} %reduce-scatter.4.cloned.1.call-done) | data formatting | bytes 131072
  406.2 2.8 copy.24
  408.9 16.3 %all-to-all-start.2 = ((bf16[64,4,128]{2,1,0:T(4,128)(2,1)}), bf16[64,4,128]{2,1,0:T(4,128)(2,1)S(1)}, u32[]{:S(2)}, u32[]{:S(2)}) async-start(bf16[64,4,128]{2,1,0:T(4,128)(2,1)} %copy.24), calls=%async_computation.2 | async-start | bytes 131072 | tf_op jit(solution)/shard_map/all_to_all | solution.py:132
  425.3 1.9 fusion.2
  427.2 2.1 fusion.3
  429.3 10.6 %all-to-all-done.2 = bf16[64,4,128]{2,1,0:T(4,128)(2,1)S(1)} async-done(((bf16[64,4,128]{2,1,0:T(4,128)(2,1)}), bf16[64,4,128]{2,1,0:T(4,128)(2,1)S(1)}, u32[]{:S(2)}, u32[]{:S(2)}) %all-to-all-start.2) | async-done | bytes 65568 | tf_op jit(solution)/shard_map/all_to_all | solution.py:132
  439.9 0.7 convolution_convert_fusion.2
  (46 shorter events, 1.9 us)
Async XLA Ops:
  7.2 2.9 copy-start
  7.2 104.6 %copy-start.3 = (bf16[1,2048,96]{1,2,0:T(8,128)(2,1)S(1)}, bf16[1,2048,96]{1,2,0:T(8,128)(2,1)}, u32[]{:S(2)}) copy-start(bf16[1,2048,96]{1,2,0:T(8,128)(2,1)} %param.16) | copy-start | bytes 1179652
  7.2 102.8 %all-gather.5.cloned.1.call-start = ((), (), s32[]{:S(2)}) async-start(), calls=%async_computation.5 | async-start | bytes 1114112 | tf_op jit(solution)/shard_map/all_gather | solution.py:105
  46.6 132.2 %all-gather.3.cloned.1.call-start = ((), (), s32[]{:S(2)}) async-start(), calls=%async_computation.4 | async-start | bytes 1114112 | tf_op jit(solution)/shard_map/all_gather | solution.py:106
  47.5 131.4 %copy-start.12 = (bf16[1,96,2048]{2,1,0:T(8,128)(2,1)S(1)}, bf16[1,96,2048]{2,1,0:T(8,128)(2,1)}, u32[]{:S(2)}) copy-start(bf16[1,96,2048]{2,1,0:T(8,128)(2,1)} %param.18) | copy-start | bytes 1179652
  67.6 333.3 %reduce-scatter.4.cloned.1.call-start = ((), (), s32[]{:S(2)}) async-start(), calls=%async_computation.6 | async-start | bytes 1114112
  67.6 12.4 %collective-permute-start.1 = (bf16[2048,96]{0,1:T(8,128)(2,1)}, bf16[2048,96]{0,1:T(8,128)(2,1)S(1)}, u32[]{:S(2)}, u32[]{:S(2)}) collective-permute-start(bf16[2048,96]{0,1:T(8,128)(2,1)} %bitcast.61), channel_id=1, source_target_pairs={{0,512},{512,0},{16,528},{528,16},{32,544},{544,32},{48,560},{560,... | collective-permute-start | bytes 1179656 | tf_op jit(solution)/shard_map/ppermute | solution.py:18
  69.7 42.1 %collective-permute-start.2 = (bf16[2048,96]{0,1:T(8,128)(2,1)}, bf16[2048,96]{0,1:T(8,128)(2,1)S(1)}, u32[]{:S(2)}, u32[]{:S(2)}) collective-permute-start(bf16[2048,96]{0,1:T(8,128)(2,1)} %bitcast.62), channel_id=1, source_target_pairs={{0,512},{512,0},{16,528},{528,16},{32,544},{544,32},{48,560},{560,... | collective-permute-start | bytes 1179656 | tf_op jit(solution)/shard_map/ppermute | solution.py:18
  72.9 40.6 %collective-permute-start = (bf16[96,2048]{1,0:T(8,128)(2,1)}, bf16[96,2048]{1,0:T(8,128)(2,1)S(1)}, u32[]{:S(2)}, u32[]{:S(2)}) collective-permute-start(bf16[96,2048]{1,0:T(8,128)(2,1)} %bitcast.70), channel_id=1, source_target_pairs={{0,512},{512,0},{16,528},{528,16},{32,544},{544,32},{48,560},{560,... | collective-permute-start | bytes 1179656 | tf_op jit(solution)/shard_map/ppermute | solution.py:18
  111.7 68.8 %copy-start.7 = (f32[256,96]{0,1:T(8,128)}, f32[256,96]{0,1:T(8,128)S(1)}, u32[]{:S(2)}) copy-start(f32[256,96]{0,1:T(8,128)S(1)} %fusion.8) | copy-start | bytes 294916
  111.8 68.8 %copy-start.2 = (bf16[1,2048,96]{1,2,0:T(8,128)(2,1)S(1)}, bf16[1,2048,96]{1,2,0:T(8,128)(2,1)}, u32[]{:S(2)}) copy-start(bf16[1,2048,96]{1,2,0:T(8,128)(2,1)} %param.17) | copy-start | bytes 1179652
  113.6 67.4 %copy-start.9 = (f32[256,96]{0,1:T(8,128)}, f32[256,96]{0,1:T(8,128)S(1)}, u32[]{:S(2)}) copy-start(f32[256,96]{0,1:T(8,128)S(1)} %fusion.9) | copy-start | bytes 294916
  180.5 0.6 copy-start.6
  234.9 63.6 %copy-start.4 = (bf16[1,2048,96]{1,2,0:T(8,128)(2,1)S(1)}, bf16[1,2048,96]{1,2,0:T(8,128)(2,1)}, u32[]{:S(2)}) copy-start(bf16[1,2048,96]{1,2,0:T(8,128)(2,1)} %param.19) | copy-start | bytes 1179652
  234.9 66.6 %copy-start.5 = (bf16[1,2048,96]{1,2,0:T(8,128)(2,1)S(1)}, bf16[1,2048,96]{1,2,0:T(8,128)(2,1)}, u32[]{:S(2)}) copy-start(bf16[1,2048,96]{1,2,0:T(8,128)(2,1)} %param.20) | copy-start | bytes 1179652
  234.9 73.6 %copy-start.1 = (bf16[256,2048]{1,0:T(8,128)(2,1)S(1)}, bf16[256,2048]{1,0:T(8,128)(2,1)}, u32[]{:S(2)}) copy-start(bf16[256,2048]{1,0:T(8,128)(2,1)} %all-gather.5.cloned.1.call-done) | copy-start | bytes 3145732
  298.5 9.9 %collective-permute-start.3 = (bf16[2048,96]{0,1:T(8,128)(2,1)S(1)}, bf16[2048,96]{0,1:T(8,128)(2,1)S(1)}, u32[]{:S(2)}, u32[]{:S(2)}) collective-permute-start(bf16[2048,96]{0,1:T(8,128)(2,1)S(1)} %bitcast.63), channel_id=1, source_target_pairs={{0,512},{512,0},{16,528},{528,16},{32,544},{544,32},{48,560},{560,... | collective-permute-start | bytes 1179656 | tf_op jit(solution)/shard_map/ppermute | solution.py:18
  301.4 123.8 %collective-permute-start.4 = (bf16[2048,96]{0,1:T(8,128)(2,1)S(1)}, bf16[2048,96]{0,1:T(8,128)(2,1)}, u32[]{:S(2)}, u32[]{:S(2)}) collective-permute-start(bf16[2048,96]{0,1:T(8,128)(2,1)S(1)} %bitcast.64), channel_id=1, source_target_pairs={{0,512},{512,0},{16,528},{528,16},{32,544},{544,32},{48,560},{560,... | collective-permute-start | bytes 1179656 | tf_op jit(solution)/shard_map/ppermute | solution.py:18
  303.8 123.4 %collective-permute-start.5 = (bf16[96,2048]{1,0:T(8,128)(2,1)}, bf16[96,2048]{1,0:T(8,128)(2,1)}, u32[]{:S(2)}, u32[]{:S(2)}) collective-permute-start(bf16[96,2048]{1,0:T(8,128)(2,1)} %bitcast.12), channel_id=1, source_target_pairs={{0,512},{512,0},{16,528},{528,16},{32,544},{544,32},{48,560},{560,... | collective-permute-start | bytes 1179656 | tf_op jit(solution)/shard_map/ppermute | solution.py:18
  408.9 18.3 %copy-start.8 = (f32[256,96]{0,1:T(8,128)S(1)}, f32[256,96]{0,1:T(8,128)}, u32[]{:S(2)}) copy-start(f32[256,96]{0,1:T(8,128)} %copy-done.7) | copy-start | bytes 294916
  408.9 18.3 %copy-start.10 = (f32[256,96]{0,1:T(8,128)S(1)}, f32[256,96]{0,1:T(8,128)}, u32[]{:S(2)}) copy-start(f32[256,96]{0,1:T(8,128)} %copy-done.9) | copy-start | bytes 294916
  408.9 18.3 %copy-start.11 = (bf16[256,2048]{1,0:T(8,128)(2,1)S(1)}, bf16[256,2048]{1,0:T(8,128)(2,1)}, u32[]{:S(2)}) copy-start(bf16[256,2048]{1,0:T(8,128)(2,1)} %all-gather.3.cloned.1.call-done) | copy-start | bytes 3145732
  408.9 31.0 %all-to-all-start.2 = ((bf16[64,4,128]{2,1,0:T(4,128)(2,1)}), bf16[64,4,128]{2,1,0:T(4,128)(2,1)S(1)}, u32[]{:S(2)}, u32[]{:S(2)}) async-start(bf16[64,4,128]{2,1,0:T(4,128)(2,1)} %copy.24), calls=%async_computation.2 | async-start | bytes 131072 | tf_op jit(solution)/shard_map/all_to_all | solution.py:132
Sparse Core Ops, SparseCore 0:
  46.8 63.1 all-gather.4
  114.1 64.6 all-gather.2
  298.6 102.2 reduce-scatter.3
where the time goes:
time: 448 us; the launch traced here: 447 us
  waiting for transfers between devices  203 us (45%)
  local copies, waits for them, and re-layouts  127 us (28%)
  blocking collectives  55.3 us (12%)
  starting transfers between devices  32 us (7%)
  between operations  14.7 us (3%)
  matrix products  13.2 us (3%)
    unnamed x32, local copies, waits for them, and re-layouts  126 us
    unnamed x4, waiting for transfers between devices  91.4 us
    all_gather x1, waiting for transfers between devices, on_device(): lax.all_gather(dy_recv, 'hidden', axis=1, tiled=True)  65.2 us
    all_to_all x1, blocking collectives, on_device(): lax.all_to_all(x_send.reshape(expert_count, capacity, slice_width), 'expe...  36.3 us
    all_gather x1, waiting for transfers between devices, on_device(): lax.all_gather(x_recv, 'hidden', axis=1, tiled=True)  29.9 us
    all_to_all x1, blocking collectives, on_device(): lax.all_to_all(dy_send.reshape(expert_count, capacity, slice_width), 'exp...  19 us
    all_to_all x1, starting transfers between devices, on_device(): lax.all_to_all(summed.astype(jnp.bfloat16), 'expert', split_axis=0, conca...  16.3 us
    ppermute x6, starting transfers between devices, partner_2(): return lax.ppermute(block, axis, route)  15.5 us
  transfers between devices with their start and end apart: 10, of which 6 were waited for; matrix products, arithmetic and copies ran while one was open for 4% of the time, Pallas kernels for 0%

commit v1 on v0

--- a/solution.py
+++ b/solution.py
@@ -55,24 +55,14 @@
     expert_count = lax.axis_size("expert")
     tok_rows, top_count = expert_ids.shape
     capacity = min(tok_rows, 2 * tok_rows * top_count // expert_count)
-    half = expert_count // 2
     pair_bit = expert_count.bit_length() - 2
     experts_iota = jnp.arange(expert_count, dtype=jnp.int32)
     my_slot = lax.axis_index("expert")
     swapping = jnp.sum(jnp.where(experts_iota == my_slot, relocate, 0)) == 1
-    partner = (experts_iota + half) % expert_count
-    arrived = partner_2(
-        (w_gate[0], w_up[0], w_down[0], moment_gate[0], moment_up[0], moment_down[0]),
-        "expert",
-        pair_bit,
-    )
-    resident = (w_gate[0], w_up[0], w_down[0], moment_gate[0], moment_up[0], moment_down[0])
-    chosen = [jnp.where(swapping, incoming, kept) for incoming, kept in zip(arrived, resident)]
-    gate_now, up_now, down_now = (chosen[0], chosen[1], chosen[2])
-    moments_now = (chosen[3], chosen[4], chosen[5])
-    destination = jnp.where(relocate == 1, partner, experts_iota)
+    gate_now, up_now, down_now = (w_gate[0], w_up[0], w_down[0])
+    moments_now = (moment_gate[0], moment_up[0], moment_down[0])
     placement, weighted = routing_matrices(
-        expert_ids, gate_probs, destination, capacity, expert_count
+        expert_ids, gate_probs, experts_iota, capacity, expert_count
     )
     rows_count = expert_count * capacity
     slice_width = tokens.shape[1]
@@ -83,28 +73,17 @@
     dy_send = jnp.dot(
         weighted, out_cotangent.astype(jnp.float32), precision=lax.Precision.HIGHEST
     ).astype(jnp.bfloat16)
-    x_recv, dy_recv = (
-        lax.all_to_all(
+    both = jnp.stack(
+        [
             x_send.reshape(expert_count, capacity, slice_width),
-            "expert",
-            split_axis=0,
-            concat_axis=0,
-            tiled=True,
-        ),
-        lax.all_to_all(
             dy_send.reshape(expert_count, capacity, slice_width),
-            "expert",
-            split_axis=0,
-            concat_axis=0,
-            tiled=True,
-        ),
+        ],
+        axis=1,
     )
-    x_recv = x_recv.reshape(rows_count, slice_width)
-    dy_recv = dy_recv.reshape(rows_count, slice_width)
-    x_full, dy_full = (
-        lax.all_gather(x_recv, "hidden", axis=1, tiled=True),
-        lax.all_gather(dy_recv, "hidden", axis=1, tiled=True),
-    )
+    both = lax.all_to_all(both, "expert", split_axis=0, concat_axis=0, tiled=True)
+    both = jnp.swapaxes(both, 0, 1).reshape(2 * rows_count, slice_width)
+    both = lax.all_gather(both, "hidden", axis=1, tiled=True)
+    x_full, dy_full = both[:rows_count], both[rows_count:]
     gate_pre = jnp.dot(x_full, gate_now, preferred_element_type=jnp.float32)
     up_pre = jnp.dot(x_full, up_now, preferred_element_type=jnp.float32)
     back = lax.dot_general(dy_full, down_now, UNIT_DIMS, preferred_element_type=jnp.float32)
@@ -116,19 +95,22 @@
     grad_gate = lax.dot_general(x_full, d_gate, ROW_DIMS, preferred_element_type=jnp.float32)
     grad_up = lax.dot_general(x_full, d_up, ROW_DIMS, preferred_element_type=jnp.float32)
     grad_down = lax.dot_general(hidden, dy_full, ROW_DIMS, preferred_element_type=jnp.float32)
-    partial_value = lax.dot_general(d_gate, gate_now, UNIT_DIMS, preferred_element_type=jnp.float32)
+    partial_value = lax.dot_general(gate_now, d_gate, UNIT_DIMS, preferred_element_type=jnp.float32)
     partial_value = partial_value + lax.dot_general(
-        d_up, up_now, UNIT_DIMS, preferred_element_type=jnp.float32
+        up_now, d_up, UNIT_DIMS, preferred_element_type=jnp.float32
     )
     fresh_gate = update_moment(moments_now[0], grad_gate)
     fresh_up = update_moment(moments_now[1], grad_up)
     fresh_down = update_moment(moments_now[2], grad_down)
+    arrived = partner_2((fresh_gate, fresh_up, fresh_down), "expert", pair_bit)
+    fresh_gate, fresh_up, fresh_down = [
+        jnp.where(swapping, incoming, kept)
+        for incoming, kept in zip(arrived, (fresh_gate, fresh_up, fresh_down))
+    ]
     summed = lax.psum_scatter(
-        partial_value.reshape(expert_count, capacity, model_width).astype(jnp.bfloat16),
-        "hidden",
-        scatter_dimension=2,
-        tiled=True,
+        partial_value.astype(jnp.bfloat16), "hidden", scatter_dimension=0, tiled=True
     ).astype(jnp.float32)
+    summed = summed.T.reshape(expert_count, capacity, slice_width)
     returned = lax.all_to_all(
         summed.astype(jnp.bfloat16), "expert", split_axis=0, concat_axis=0, tiled=True
     ).astype(summed.dtype)

time: 448 us -> 268 us (0.60)
  local copies, waits for them, and re-layouts: 127 us -> 5.4 us
  waiting for transfers between devices: 203 us -> 171 us
  blocking collectives: 55.3 us -> 38.8 us
  starting transfers between devices: 32 us -> 23.5 us
    unnamed x32 -> x26, local copies, waits for them, and re-layouts: 126 us -> 4.53 us
    all_gather x2 -> x1, waiting for transfers between devices: 95.1 us -> 67.2 us  [on_device(): both = lax.all_gather(both, 'hidden', axis=1, tiled=True)]
    all_to_all x2 -> x1, blocking collectives: 55.3 us -> 38.8 us  [on_device(): lax.all_to_all(both, 'expert', split_axis=0, concat_axis=0, tiled=True)]
    unnamed x4 -> x3, waiting for transfers between devices: 91.4 us -> 81.2 us
    ppermute x6 -> x3, starting transfers between devices: 15.5 us -> 7.21 us  [partner_2(): return lax.ppermute(block, axis, route)]
    ppermute x6 -> x3, waiting for transfers between devices: 6.09 us -> 9.2 us  [partner_2(): return lax.ppermute(block, axis, route)]
  transfers between devices with their start and end apart: 10 -> 6, of which waited for: 6 -> 5; matrix products, arithmetic and copies ran while one was open for 4% -> 3% of each run, Pallas kernels for 0% -> 0%
where the time goes in v1:
time: 268 us
  waiting for transfers between devices  171 us (64%)
  blocking collectives  38.8 us (14%)
  starting transfers between devices  23.5 us (9%)
  between operations  15 us (6%)
  matrix products  9.71 us (4%)
  local copies, waits for them, and re-layouts  5.4 us (2%)
  other arithmetic  3.79 us (1%)
    unnamed x3, waiting for transfers between devices  81.2 us
    all_gather x1, waiting for transfers between devices, on_device(): both = lax.all_gather(both, 'hidden', axis=1, tiled=True)  67.2 us
    all_to_all x1, blocking collectives, on_device(): lax.all_to_all(both, 'expert', split_axis=0, concat_axis=0, tiled=True)  38.8 us
    all_to_all x1, starting transfers between devices, on_device(): lax.all_to_all(summed.astype(jnp.bfloat16), 'expert', split_axis=0, conca...  16.2 us
    all_to_all x1, waiting for transfers between devices, on_device(): lax.all_to_all(summed.astype(jnp.bfloat16), 'expert', split_axis=0, conca...  13.8 us
    ppermute x3, waiting for transfers between devices, partner_2(): return lax.ppermute(block, axis, route)  9.2 us
    ppermute x3, starting transfers between devices, partner_2(): return lax.ppermute(block, axis, route)  7.21 us
  transfers between devices with their start and end apart: 6, of which 5 were waited for; matrix products, arithmetic and copies ran while one was open for 3% of the time, Pallas kernels for 0%

profile of v1, /device:TPU:1, one launch (start us, length us, event | category | flops | bytes accessed | tf_op | source)
XLA Modules:
  0.0 267.6 jit_solution(10308674189723796018)
XLA Ops:
  7.2 0.8 copy.28
  8.1 0.8 copy.29
  9.0 0.2 reduce_window_sum.11
  9.2 0.2 select_reduce_fusion.2
  9.7 1.0 convolution_convert_fusion
  10.7 0.9 convolution_convert_fusion.1
  11.7 38.8 %all_to_all.10 = bf16[64,2,4,128]{3,2,1,0:T(4,128)(2,1)S(1)} all-to-all(bf16[64,2,4,128]{3,2,1,0:T(4,128)(2,1)S(1)} %pad_maximum_fusion), channel_id=1, replica_groups=mesh['expert'=64,'hidden'=16] {'expert'}, dimensions={0} | all-to-all | bytes 262144 | tf_op jit(solution)/shard_map/all_to_all | solution.py:83
  50.6 0.7 copy.32
  51.3 67.2 %all-gather.2.cloned.1.call-done = bf16[512,2048]{1,0:T(8,128)(2,1)} async-done(((bf16[512,128]{1,0:T(8,128)(2,1)}), bf16[512,2048]{1,0:T(8,128)(2,1)}) %all-gather.2.cloned.1.call-update) | async-done | bytes 2097168 | tf_op jit(solution)/shard_map/all_gather | solution.py:85
  118.6 1.8 fusion.13
  120.4 1.7 fusion.15
  122.2 0.5 multiply_convert_fusion.1
  122.6 0.5 fusion.17
  123.1 0.5 fusion.1
  123.6 1.3 copy.33
  125.0 0.6 fusion.27
  126.3 1.6 fusion.6
  127.9 1.9 collective-permute-start
  129.8 0.3 fusion.7
  130.1 3.4 %collective-permute-start.1 = (bf16[2048,96]{0,1:T(8,128)(2,1)S(1)}, bf16[2048,96]{0,1:T(8,128)(2,1)S(1)}, u32[]{:S(2)}, u32[]{:S(2)}) collective-permute-start(bf16[2048,96]{0,1:T(8,128)(2,1)S(1)} %fusion.7), channel_id=1, source_target_pairs={{0,512},{512,0},{16,528},{528,16},{32,544},{544,32},{48,560},{560,... | collective-permute-start | bytes 1179656 | tf_op jit(solution)/shard_map/ppermute | solution.py:18
  133.5 0.3 fusion.5
  133.8 1.9 collective-permute-start.2
  135.8 1.6 collective-permute-done
  137.3 0.8 select_bitcast_fusion.2
  138.1 7.6 %collective-permute-done.1 = bf16[2048,96]{0,1:T(8,128)(2,1)S(1)} collective-permute-done((bf16[2048,96]{0,1:T(8,128)(2,1)S(1)}, bf16[2048,96]{0,1:T(8,128)(2,1)S(1)}, u32[]{:S(2)}, u32[]{:S(2)}) %collective-permute-start.1) | collective-permute-done | bytes 393248 | tf_op jit(solution)/shard_map/ppermute | solution.py:18
  145.8 0.8 select_bitcast_fusion.1
  146.6 81.2 %reduce-scatter.4.cloned.1.call-done = bf16[128,256]{1,0:T(8,128)(2,1)} async-done(((bf16[2048,256]{1,0:T(8,128)(2,1)}), bf16[128,256]{1,0:T(8,128)(2,1)}) %reduce-scatter.4.cloned.1.call-update) | async-done | bytes 65552
  227.8 1.6 copy.34
  229.3 16.2 %all-to-all-start.1 = ((bf16[64,4,128]{2,1,0:T(4,128)(2,1)}), bf16[64,4,128]{2,1,0:T(4,128)(2,1)S(1)}, u32[]{:S(2)}, u32[]{:S(2)}) async-start(bf16[64,4,128]{2,1,0:T(4,128)(2,1)} %bitcast.11), calls=%async_computation.1 | async-start | bytes 131072 | tf_op jit(solution)/shard_map/all_to_all | solution.py:114
  245.5 0.8 select_bitcast_fusion
  246.3 13.8 %all-to-all-done.1 = bf16[64,4,128]{2,1,0:T(4,128)(2,1)S(1)} async-done(((bf16[64,4,128]{2,1,0:T(4,128)(2,1)}), bf16[64,4,128]{2,1,0:T(4,128)(2,1)S(1)}, u32[]{:S(2)}, u32[]{:S(2)}) %all-to-all-start.1) | async-done | bytes 65568 | tf_op jit(solution)/shard_map/all_to_all | solution.py:114
  260.1 0.7 convolution_convert_fusion.2
  (34 shorter events, 0.8 us)
Async XLA Ops:
  7.2 111.4 %copy-start = (bf16[1,2048,96]{1,2,0:T(8,128)(2,1)S(1)}, bf16[1,2048,96]{1,2,0:T(8,128)(2,1)}, u32[]{:S(2)}) copy-start(bf16[1,2048,96]{1,2,0:T(8,128)(2,1)} %param.16) | copy-start | bytes 1179652
  7.2 113.2 %copy-start.1 = (bf16[1,2048,96]{1,2,0:T(8,128)(2,1)S(1)}, bf16[1,2048,96]{1,2,0:T(8,128)(2,1)}, u32[]{:S(2)}) copy-start(bf16[1,2048,96]{1,2,0:T(8,128)(2,1)} %param.17) | copy-start | bytes 1179652
  7.2 111.4 %all-gather.2.cloned.1.call-start = ((), (), s32[]{:S(2)}) async-start(), calls=%async_computation.3 | async-start | bytes 2228224 | tf_op jit(solution)/shard_map/all_gather | solution.py:85
  11.7 110.4 %copy-start.4 = (bf16[1,96,2048]{2,1,0:T(8,128)(2,1)S(1)}, bf16[1,96,2048]{2,1,0:T(8,128)(2,1)}, u32[]{:S(2)}) copy-start(bf16[1,96,2048]{2,1,0:T(8,128)(2,1)} %param.18) | copy-start | bytes 1179652
  51.3 176.5 %reduce-scatter.4.cloned.1.call-start = ((), (), s32[]{:S(2)}) async-start(), calls=%async_computation.4 | async-start | bytes 1114112
  118.6 3.6 %copy-start.2 = (bf16[512,2048]{1,0:T(8,128)(2,1)S(1)}, bf16[512,2048]{1,0:T(8,128)(2,1)}, u32[]{:S(2)}) copy-start(bf16[512,2048]{1,0:T(8,128)(2,1)} %all-gather.2.cloned.1.call-done) | copy-start | bytes 6291460
  122.2 0.9 copy-start.9
  123.6 1.4 copy-start.8
  123.6 2.7 %copy-start.5 = (bf16[1,2048,96]{1,2,0:T(8,128)(2,1)S(1)}, bf16[1,2048,96]{1,2,0:T(8,128)(2,1)}, u32[]{:S(2)}) copy-start(bf16[1,2048,96]{1,2,0:T(8,128)(2,1)} %param.19) | copy-start | bytes 1179652
  123.6 6.2 %copy-start.6 = (bf16[1,2048,96]{1,2,0:T(8,128)(2,1)S(1)}, bf16[1,2048,96]{1,2,0:T(8,128)(2,1)}, u32[]{:S(2)}) copy-start(bf16[1,2048,96]{1,2,0:T(8,128)(2,1)} %param.20) | copy-start | bytes 1179652
  124.9 4.9 %copy-start.3 = (bf16[512,2048]{1,0:T(8,128)(2,1)S(1)}, bf16[512,2048]{1,0:T(8,128)(2,1)}, u32[]{:S(2)}) copy-start(bf16[512,2048]{1,0:T(8,128)(2,1)} %all-gather.2.cloned.1.call-done) | copy-start | bytes 6291460
  126.3 7.3 %copy-start.7 = (bf16[1,96,2048]{2,1,0:T(8,128)(2,1)S(1)}, bf16[1,96,2048]{2,1,0:T(8,128)(2,1)}, u32[]{:S(2)}) copy-start(bf16[1,96,2048]{2,1,0:T(8,128)(2,1)} %param.21) | copy-start | bytes 1179652
  126.3 7.3 %copy-start.10 = (f32[256,96]{0,1:T(8,128)S(1)}, f32[256,96]{0,1:T(8,128)}, u32[]{:S(2)}) copy-start(f32[256,96]{0,1:T(8,128)} %copy-done.9) | copy-start | bytes 294916
  127.9 9.5 %collective-permute-start = (bf16[2048,96]{0,1:T(8,128)(2,1)S(1)}, bf16[2048,96]{0,1:T(8,128)(2,1)S(1)}, u32[]{:S(2)}, u32[]{:S(2)}) collective-permute-start(bf16[2048,96]{0,1:T(8,128)(2,1)S(1)} %fusion.6), channel_id=1, source_target_pairs={{0,512},{512,0},{16,528},{528,16},{32,544},{544,32},{48,560},{560,... | collective-permute-start | bytes 1179656 | tf_op jit(solution)/shard_map/ppermute | solution.py:18
  130.1 15.6 %collective-permute-start.1 = (bf16[2048,96]{0,1:T(8,128)(2,1)S(1)}, bf16[2048,96]{0,1:T(8,128)(2,1)S(1)}, u32[]{:S(2)}, u32[]{:S(2)}) collective-permute-start(bf16[2048,96]{0,1:T(8,128)(2,1)S(1)} %fusion.7), channel_id=1, source_target_pairs={{0,512},{512,0},{16,528},{528,16},{32,544},{544,32},{48,560},{560,... | collective-permute-start | bytes 1179656 | tf_op jit(solution)/shard_map/ppermute | solution.py:18
  133.8 111.7 %collective-permute-start.2 = (bf16[96,2048]{1,0:T(8,128)(2,1)S(1)}, bf16[96,2048]{1,0:T(8,128)(2,1)S(1)}, u32[]{:S(2)}, u32[]{:S(2)}) collective-permute-start(bf16[96,2048]{1,0:T(8,128)(2,1)S(1)} %fusion.5), channel_id=1, source_target_pairs={{0,512},{512,0},{16,528},{528,16},{32,544},{544,32},{48,560},{560,... | collective-permute-start | bytes 1179656 | tf_op jit(solution)/shard_map/ppermute | solution.py:18
  229.3 30.8 %all-to-all-start.1 = ((bf16[64,4,128]{2,1,0:T(4,128)(2,1)}), bf16[64,4,128]{2,1,0:T(4,128)(2,1)S(1)}, u32[]{:S(2)}, u32[]{:S(2)}) async-start(bf16[64,4,128]{2,1,0:T(4,128)(2,1)} %bitcast.11), calls=%async_computation.1 | async-start | bytes 131072 | tf_op jit(solution)/shard_map/all_to_all | solution.py:114
Sparse Core Ops, SparseCore 0:
  51.4 67.1 all-gather.1
  125.1 102.6 reduce-scatter.3

commit v2 on v1

v2 whole, which is shorter than its diff:
```python
import functools

import jax
import jax.numpy as jnp
from jax import lax
from jax.experimental import pallas as pl
from jax.experimental.pallas import tpu as pltpu
from jax.sharding import PartitionSpec as P

MOMENT_DECAY = 0.9
CAPACITY = 4
LANES = 128
SIDE = 4
MESH = pl.DeviceIdType.MESH
NT = (((1,), (1,)), ((), ()))
NN = (((1,), (0,)), ((), ()))


def routing(expert_ids, gate_probs, expert_count):
    tok_rows, top_count = expert_ids.shape
    flat_ids = expert_ids.reshape(tok_rows * top_count)
    experts_iota = jnp.arange(expert_count, dtype=jnp.int32)
    onehot = (flat_ids[:, None] == experts_iota[None, :]).astype(jnp.int32)
    ranks = jnp.sum((jnp.cumsum(onehot, axis=0) - onehot) * onehot, axis=1)
    slots = (flat_ids * (2 * CAPACITY) + ranks).reshape(tok_rows, top_count)
    slot_iota = jnp.arange(expert_count * 2 * CAPACITY, dtype=jnp.int32)
    take_x = slots[None, :, :] == slot_iota[:, None, None]
    take_dy = slots[None, :, :] + CAPACITY == slot_iota[:, None, None]
    placement = jnp.any(take_x, axis=2).astype(jnp.bfloat16)
    weighted = jnp.sum(jnp.where(take_dy, gate_probs[None, :, :], 0.0), axis=2)
    back_slots = slots[:, :, None] == slot_iota[None, None, :]
    collect = jnp.any(back_slots, axis=1).astype(jnp.bfloat16)
    return placement, weighted, collect


def dot(a, b, dims):
    return lax.dot_general(a, b, dims, preferred_element_type=jnp.float32)


def kernel(
    send_ref,
    collect_ref,
    wg_ref,
    wu_ref,
    wd_ref,
    mg_ref,
    mu_ref,
    md_ref,
    tok_ref,
    own_ref,
    got_ref,
    w,
    m,
    g,
    acc,
    sides,
    p,
    buf_a,
    buf_b,
    buf_c,
    buf_d,
    tmp_r,
    tmp_l,
    q,
    y_a,
    y_b,
    y_c,
    y_d,
    y_r,
    y_l,
    back,
    ret,
    load_sem,
    a2a_sem,
    gs_sem,
    gr_sem,
    ps_sem,
    pr_sem,
    ms_sem,
    mr_sem,
    ret_sem,
):
    count = send_ref.shape[0]
    units = wg_ref.shape[0]
    wide = count * 2 * CAPACITY
    rows = count * CAPACITY
    half = count // 2
    e = lax.axis_index("expert")
    hid = lax.axis_index("hidden")
    x, y = lax.div(hid, SIDE), lax.rem(hid, SIDE)

    def h_at(dx, dy):
        return lax.rem(x + dx, SIDE) * SIDE + lax.rem(y + dy, SIDE)

    def peer(de, dx, dy):
        return (lax.rem(e + de, count), h_at(dx, dy))

    x_right, x_left = peer(0, 1, 0), peer(0, 3, 0)
    y_right, y_left = peer(0, 0, 1), peer(0, 0, 3)
    partner = peer(half, 0, 0)

    loads = [
        pltpu.make_async_copy(src, dst.at[pl.ds(i * units, units)], load_sem.at[j * 3 + i])
        for j, (dst, group) in enumerate(
            ((w, (wg_ref, wu_ref, wd_ref)), (m, (mg_ref, mu_ref, md_ref)))
        )
        for i, src in enumerate(group)
    ]
    for load in loads:
        load.start()

    barrier = pltpu.get_barrier_semaphore()

    def greet(i, carry):
        pl.semaphore_signal(barrier, inc=1, device_id=peer(i, 0, 0), device_id_type=MESH)
        return carry

    lax.fori_loop(1, count, greet, 0)
    for near in (x_right, x_left, y_right, y_left):
        pl.semaphore_signal(barrier, inc=1, device_id=near, device_id_type=MESH)
    pl.semaphore_wait(barrier, count - 1 + 4)

    def remote(src, dst, ssem, rsem, to):
        return pltpu.make_async_remote_copy(
            src_ref=src,
            dst_ref=dst,
            send_sem=ssem,
            recv_sem=rsem,
            device_id=to,
            device_id_type=MESH,
        )

    me = h_at(0, 0)

    def deal(i, carry):
        to = peer(i, 0, 0)
        remote(send_ref.at[to[0]], g.at[me, e], a2a_sem.at[0], a2a_sem.at[1], to).start()
        return carry

    lax.fori_loop(1, count, deal, 0)
    keep = pltpu.make_async_copy(send_ref.at[e], g.at[me, e], a2a_sem.at[2])
    keep.start()
    keep.wait()
    dealt = remote(
        send_ref.at[pl.ds(0, count - 1)],
        g.at[me, pl.ds(0, count - 1)],
        a2a_sem.at[0],
        a2a_sem.at[1],
        x_right,
    )
    dealt.wait_recv()

    sent = []

    def push(src, dst, sems, n, to):
        copy = remote(src, dst, sems[0].at[n], sems[1].at[n], to)
        copy.start()
        sent.append(copy)
        return copy

    gs = (gs_sem, gr_sem)

    def x_out(n, dy):
        h = h_at(0, dy)
        return (
            push(g.at[h], g.at[h], gs, 4 + 4 * n, x_right),
            push(g.at[h], g.at[h], gs, 5 + 4 * n, x_left),
        )

    def x_forward(n, dy, from_left, from_right):
        from_left.wait_recv()
        h = h_at(3, dy)
        low = g.at[h, pl.ds(0, half)]
        a = push(low, low, gs, 6 + 4 * n, x_right)
        from_right.wait_recv()
        h = h_at(1, dy)
        high = g.at[h, pl.ds(half, half)]
        b = push(high, high, gs, 7 + 4 * n, x_left)
        return a, b

    def absorb(dx, dy, first=False):
        h = h_at(dx, dy)
        cols = pl.ds(pl.multiple_of(h * LANES, LANES), LANES)
        term = dot(w[:, cols], g[h].reshape(wide, LANES), NT)
        if first:
            acc[...] = term
        else:
            acc[...] += term

    from_yl = push(g.at[me], g.at[me], gs, 0, y_right)
    from_yr = push(g.at[me], g.at[me], gs, 1, y_left)
    in0 = x_out(0, 0)
    for load in loads[:3]:
        load.wait()
    absorb(0, 0, True)
    from_yl.wait_recv()
    h = h_at(0, 3)
    low = g.at[h, pl.ds(0, half)]
    opp_low = push(low, low, gs, 2, y_right)
    in1 = x_out(1, 3)
    from_yr.wait_recv()
    h = h_at(0, 1)
    high = g.at[h, pl.ds(half, half)]
    opp_high = push(high, high, gs, 3, y_left)
    in2 = x_out(2, 1)
    fwd0 = x_forward(0, 0, *in0)
    absorb(0, 3)
    absorb(0, 1)
    opp_low.wait_recv()
    opp_high.wait_recv()
    in3 = x_out(3, 2)
    absorb(0, 2)
    absorb(3, 0)
    absorb(1, 0)
    fwd1 = x_forward(1, 3, *in1)
    absorb(3, 3)
    absorb(1, 3)
    fwd2 = x_forward(2, 1, *in2)
    absorb(3, 1)
    absorb(1, 1)
    fwd3 = x_forward(3, 2, *in3)
    absorb(3, 2)
    absorb(1, 2)
    for dy, arrivals in ((0, fwd0), (3, fwd1), (1, fwd2), (2, fwd3)):
        for copy in arrivals:
            copy.wait_recv()
        absorb(2, dy)

    gate = acc[pl.ds(0, units), :]
    up = acc[pl.ds(units, units), :]
    down = pltpu.roll(acc[pl.ds(2 * units, units), :], wide - CAPACITY, 1)
    lane = lax.broadcasted_iota(jnp.int32, (units, wide), 1)
    is_x = jnp.bitwise_and(lane, 2 * CAPACITY - 1) < CAPACITY
    sig = jax.nn.sigmoid(gate)
    act = gate * sig
    d_gate = down * up * sig * (1.0 + gate * (1.0 - sig))
    d_up = down * act
    hidden = pltpu.roll(jnp.where(is_x, act * up, 0.0), CAPACITY, 1)
    sides[pl.ds(0, units), :] = jnp.where(is_x, d_gate, 0.0).astype(jnp.bfloat16)
    sides[pl.ds(units, units), :] = jnp.where(is_x, d_up, 0.0).astype(jnp.bfloat16)
    sides[pl.ds(2 * units, units), :] = hidden.astype(jnp.bfloat16)

    row = lax.broadcasted_iota(jnp.int32, (rows, wide), 0)
    col = lax.broadcasted_iota(jnp.int32, (rows, wide), 1)
    slot = (row // CAPACITY) * (2 * CAPACITY) + jnp.bitwise_and(row, CAPACITY - 1)
    compact = (slot == col).astype(jnp.float32).astype(jnp.bfloat16)
    d_rows = dot(compact, sides[pl.ds(0, 2 * units), :], NT).astype(jnp.bfloat16)

    def quarter(dx):
        block = lax.rem(x + dx, SIDE)
        cols = pl.ds(pl.multiple_of(block * (SIDE * LANES), LANES), SIDE * LANES)
        value = dot(d_rows, w[pl.ds(0, 2 * units), cols], NN).astype(jnp.bfloat16)
        for j in range(SIDE):
            p[block * SIDE + j] = value[:, j * LANES : (j + 1) * LANES]
        return block * SIDE

    ps = (ps_sem, pr_sem)
    o = quarter(2)
    from_a = push(p.at[pl.ds(o, 2)], buf_a, ps, 0, x_right)
    from_b = push(p.at[pl.ds(o + 2, 2)], buf_b, ps, 1, x_left)
    r = quarter(1)
    c_high = push(p.at[pl.ds(r + 2, 2)], buf_c.at[pl.ds(2, 2)], ps, 2, x_right)
    l = quarter(3)
    d_low = push(p.at[pl.ds(l, 2)], buf_d.at[pl.ds(0, 2)], ps, 3, x_left)
    s = quarter(0)

    for load in loads[3:]:
        load.wait()

    def fresh(i):
        span = pl.ds(i * units, units)
        for k in range(SIDE * SIDE // 2):
            rhs = jnp.concatenate(
                [g[2 * k].reshape(wide, LANES), g[2 * k + 1].reshape(wide, LANES)], axis=1
            )
            grad = dot(sides[span, :], rhs, NN)
            cols = pl.ds(2 * k * LANES, 2 * LANES)
            old = m[span, cols].astype(jnp.float32)
            own_ref[span, cols] = (MOMENT_DECAY * old + (1.0 - MOMENT_DECAY) * grad).astype(
                jnp.bfloat16
            )
        return push(own_ref.at[span], got_ref.at[span], (ms_sem, mr_sem), i, partner)

    swaps = [fresh(0)]

    def add(a, b):
        return (a.astype(jnp.float32) + b.astype(jnp.float32)).astype(jnp.bfloat16)

    from_a.wait_recv()
    tmp_r[...] = add(p[pl.ds(r, 2)], buf_a[...])
    c_low = push(tmp_r, buf_c.at[pl.ds(0, 2)], ps, 4, x_right)
    from_b.wait_recv()
    tmp_l[...] = add(p[pl.ds(l + 2, 2)], buf_b[...])
    d_high = push(tmp_l, buf_d.at[pl.ds(2, 2)], ps, 5, x_left)
    for copy in (c_high, d_low, c_low, d_high):
        copy.wait_recv()
    f32 = jnp.float32
    q[...] = (
        p[pl.ds(s, SIDE)].astype(f32) + buf_c[...].astype(f32) + buf_d[...].astype(f32)
    ).astype(jnp.bfloat16)

    top, low_rows = pl.ds(0, rows // 2), pl.ds(rows // 2, rows // 2)
    yo, yr, yl = lax.rem(y + 2, SIDE), lax.rem(y + 1, SIDE), lax.rem(y + 3, SIDE)
    from_a = push(q.at[yo, top], y_a, ps, 6, y_right)
    from_b = push(q.at[yo, low_rows], y_b, ps, 7, y_left)
    c_high = push(q.at[yr, low_rows], y_c.at[low_rows], ps, 8, y_right)
    d_low = push(q.at[yl, top], y_d.at[top], ps, 9, y_left)
    from_a.wait_recv()
    y_r[...] = add(q[yr, top], y_a[...])
    c_low = push(y_r, y_c.at[top], ps, 10, y_right)
    from_b.wait_recv()
    y_l[...] = add(q[yl, low_rows], y_b[...])
    d_high = push(y_l, y_d.at[low_rows], ps, 11, y_left)
    swaps.append(fresh(1))
    for copy in (c_high, d_low, c_low, d_high):
        copy.wait_recv()
    total = (q[y].astype(f32) + y_c[...].astype(f32) + y_d[...].astype(f32)).astype(jnp.bfloat16)

    row = lax.broadcasted_iota(jnp.int32, (wide, rows), 0)
    col = lax.broadcasted_iota(jnp.int32, (wide, rows), 1)
    slot = (col // CAPACITY) * (2 * CAPACITY) + jnp.bitwise_and(col, CAPACITY - 1)
    spread = (slot == row).astype(jnp.float32).astype(jnp.bfloat16)
    back[...] = dot(spread, total, NN).astype(jnp.bfloat16).reshape(back.shape)

    def give(i, carry):
        to = peer(i, 0, 0)
        remote(back.at[to[0]], ret.at[e], ret_sem.at[0], ret_sem.at[1], to).start()
        return carry

    lax.fori_loop(1, count, give, 0)
    swaps.append(fresh(2))
    keep = pltpu.make_async_copy(back.at[e], ret.at[e], ret_sem.at[2])
    keep.start()
    keep.wait()
    given = remote(
        back.at[pl.ds(0, count - 1)],
        ret.at[pl.ds(0, count - 1)],
        ret_sem.at[0],
        ret_sem.at[1],
        x_right,
    )
    given.wait_recv()
    tok_ref[...] = dot(collect_ref[...], ret[...].reshape(wide, LANES), NN).astype(jnp.bfloat16)

    for copy in swaps:
        copy.wait_recv()
    for copy in sent:
        copy.wait_send()
    dealt.wait_send()
    given.wait_send()


def run_kernel(send, collect, weights, moments):
    count = send.shape[0]
    units, width = weights[0].shape
    wide, rows = count * 2 * CAPACITY, count * CAPACITY
    blocks = SIDE * SIDE
    bf16, f32 = jnp.bfloat16, jnp.float32
    vmem, dma = pltpu.VMEM, pltpu.SemaphoreType.DMA
    return pl.pallas_call(
        kernel,
        out_shape=(
            jax.ShapeDtypeStruct((collect.shape[0], LANES), bf16),
            jax.ShapeDtypeStruct((3 * units, width), bf16),
            jax.ShapeDtypeStruct((3 * units, width), bf16),
        ),
        in_specs=[pl.BlockSpec(memory_space=vmem)] * 2 + [pl.BlockSpec(memory_space=pl.ANY)] * 6,
        out_specs=(
            pl.BlockSpec(memory_space=vmem),
            pl.BlockSpec(memory_space=vmem),
            pl.BlockSpec(memory_space=pl.ANY),
        ),
        scratch_shapes=[
            vmem((3 * units, width), bf16),
            vmem((3 * units, width), bf16),
            vmem((blocks, count, 2 * CAPACITY, LANES), bf16),
            vmem((3 * units, wide), f32),
            vmem((3 * units, wide), bf16),
            vmem((blocks, rows, LANES), bf16),
            vmem((2, rows, LANES), bf16),
            vmem((2, rows, LANES), bf16),
            vmem((4, rows, LANES), bf16),
            vmem((4, rows, LANES), bf16),
            vmem((2, rows, LANES), bf16),
            vmem((2, rows, LANES), bf16),
            vmem((4, rows, LANES), bf16),
            vmem((rows // 2, LANES), bf16),
            vmem((rows // 2, LANES), bf16),
            vmem((rows, LANES), bf16),
            vmem((rows, LANES), bf16),
            vmem((rows // 2, LANES), bf16),
            vmem((rows // 2, LANES), bf16),
            vmem((count, 2 * CAPACITY, LANES), bf16),
            vmem((count, 2 * CAPACITY, LANES), bf16),
            dma((6,)),
            dma((3,)),
            dma((20,)),
            dma((20,)),
            dma((12,)),
            dma((12,)),
            dma((3,)),
            dma((3,)),
            dma((3,)),
        ],
        compiler_params=pltpu.CompilerParams(
            collective_id=0, has_side_effects=True, vmem_limit_bytes=48 * 1024 * 1024
        ),
        name="experts",
    )(send, collect, *weights, *moments)


def on_device(
    tokens,
    out_cotangent,
    expert_ids,
    gate_probs,
    relocate,
    w_gate,
    w_up,
    w_down,
    moment_gate,
    moment_up,
    moment_down,
):
    count = lax.axis_size("expert")
    my_slot = lax.axis_index("expert")
    experts_iota = jnp.arange(count, dtype=jnp.int32)
    swapping = jnp.sum(jnp.where(experts_iota == my_slot, relocate, 0)) == 1
    placement, weighted, collect = routing(expert_ids, gate_probs, count)
    x_part = jnp.dot(placement, tokens, preferred_element_type=jnp.float32)
    dy_part = jnp.dot(
        weighted, out_cotangent.astype(jnp.float32), precision=lax.Precision.HIGHEST
    )
    send = (x_part + dy_part).astype(jnp.bfloat16).reshape(count, 2 * CAPACITY, LANES)
    token_grad, own, got = run_kernel(
        send,
        collect,
        (w_gate[0].T, w_up[0].T, w_down[0]),
        (moment_gate[0].T, moment_up[0].T, moment_down[0]),
    )
    units = w_down.shape[1]
    fresh = [
        jnp.where(swapping, got[i * units : (i + 1) * units], own[i * units : (i + 1) * units])
        for i in range(3)
    ]
    return (token_grad, fresh[0].T[None], fresh[1].T[None], fresh[2][None])


def solution(mesh):
    return jax.shard_map(
        on_device,
        mesh=mesh,
        in_specs=(
            P("expert", "hidden"),
            P("expert", "hidden"),
            P("expert", None),
            P("expert", None),
            P(),
            P("expert", None, "hidden"),
            P("expert", None, "hidden"),
            P("expert", "hidden", None),
            P("expert", None, "hidden"),
            P("expert", None, "hidden"),
            P("expert", "hidden", None),
        ),
        out_specs=(
            P("expert", "hidden"),
            P("expert", None, "hidden"),
            P("expert", None, "hidden"),
            P("expert", "hidden", None),
        ),
        check_vma=False,
    )
```

time: 268 us -> 108 us (0.40)
  waiting for transfers between devices: 171 us -> 0 us
  Pallas kernels: 0 us -> 93.7 us
  blocking collectives: 38.8 us -> 0 us
  starting transfers between devices: 23.5 us -> 0 us
  between operations: 15 us -> 1.41 us
  matrix products: 9.71 us -> 1.33 us
    pallas_call x0 -> x1, Pallas kernels: none -> 93.7 us  [run_kernel(): pl.pallas_call(kernel, out_shape=(jax.ShapeDtypeStruct((collect.shape[0],...]
    unnamed x3 -> x0, waiting for transfers between devices: 81.2 us -> none
    all_gather x1 -> x0, waiting for transfers between devices: 67.2 us -> none  [on_device(): both = lax.all_gather(both, 'hidden', axis=1, tiled=True)]
    all_to_all x1 -> x0, blocking collectives: 38.8 us -> none  [on_device(): lax.all_to_all(both, 'expert', split_axis=0, concat_axis=0, tiled=True)]
    all_to_all x1 -> x0, starting transfers between devices: 16.2 us -> none  [on_device(): lax.all_to_all(summed.astype(jnp.bfloat16), 'expert', split_axis=0, conca...]
    all_to_all x1 -> x0, waiting for transfers between devices: 13.8 us -> none  [on_device(): lax.all_to_all(summed.astype(jnp.bfloat16), 'expert', split_axis=0, conca...]
    ppermute x3 -> x0, waiting for transfers between devices: 9.2 us -> none  [partner_2(): return lax.ppermute(block, axis, route)]
    dot_general x10 -> x1, matrix products: 8.73 us -> 0.25 us  [on_device(): x_part = jnp.dot(placement, tokens, preferred_element_type=jnp.float32)]
  transfers between devices with their start and end apart: 6 -> 0, of which waited for: 5 -> 0; matrix products, arithmetic and copies ran while one was open for 3% -> 0% of each run, Pallas kernels for 0% -> 0%
where the time goes in v2:
time: 108 us; the launch traced here: 106 us
  Pallas kernels  93.7 us (87%)
  local copies, waits for them, and re-layouts  6.27 us (6%)
  other arithmetic  3.34 us (3%)
  between operations  1.41 us (1%)
  matrix products  1.33 us (1%)
    pallas_call x1, Pallas kernels, run_kernel(): pl.pallas_call(kernel, out_shape=(jax.ShapeDtypeStruct((collect.shape[0],...  93.7 us
    unnamed x17, local copies, waits for them, and re-layouts  6.11 us

profile of v2, /device:TPU:1, one launch (start us, length us, event | category | flops | bytes accessed | tf_op | source)
XLA Modules:
  0.0 106.1 jit_solution(13355711065588325746)
XLA Ops:
  0.6 0.0 copy-start
  0.6 0.0 copy-start.2
  0.7 0.0 copy-start.1
  0.7 1.4 %fusion.5 = s32[]{:T(128)} fusion(s32[64]{0:T(128)} %param.15, s32[]{:T(128)S(6)} %axis_index.15), kind=kLoop, calls=%fused_computation.18 | loop fusion | flops 191 | bytes 264 | tf_op jit(solution)/shard_map/reduce_sum | solution.py:428
  2.7 0.8 copy.21
  3.4 0.1 eq.63
  3.5 0.8 copy.23
  4.3 0.1 fusion.4
  4.4 0.2 reduce_window_sum.11
  4.6 0.2 select_reduce_fusion.1
  4.7 0.1 reduce_sum.30
  4.8 0.2 fusion.3
  5.0 0.2 fusion.2
  5.2 0.2 select_reduce_fusion
  5.3 0.0 copy-done
  5.4 0.2 fusion.6
  5.6 1.1 %fusion.1.send_ref = bf16[64,8,128]{2,1,0:T(8,128)(2,1)S(1)} fusion(f32[512,128]{1,0:T(8,128)S(1)} %fusion.6, f32[512,16]{0,1:T(8,128)S(1)} %select_reduce_fusion, bf16[16,128]{1,0:T(8,128)(2,1)} %param.12), kind=kOutput, calls=%fused_computation.2 | convolution fusion | flops 12713984 | bytes 430080 | tf_op jit(solution)/shard_map/dot_general | solution.py:431
  6.7 0.0 copy-done.2
  6.7 0.0 copy-done.1
  6.7 0.0 copy-start.3
  6.7 1.0 copy-done.3
  7.7 0.0 copy-start.4
  7.7 1.0 copy-done.4
  8.7 0.0 copy-start.5
  8.7 1.0 copy-done.5
  9.7 0.0 copy-start.6
  9.7 1.0 copy-done.6
  10.7 93.7 %experts.1 = (bf16[16,128]{1,0:T(8,128)(2,1)S(1)}, bf16[288,2048]{1,0:T(8,128)(2,1)S(1)}, bf16[288,2048]{1,0:T(8,128)(2,1)S(1)}) custom-call(bf16[64,8,128]{2,1,0:T(8,128)(2,1)S(1)} %fusion.1.send_ref, bf16[16,512]{1,0:T(8,128)(2,1)S(1)} %convert_element_type.13.collect_ref, bf16[96,2048]{1,0:T(8,128)(2,1)S(1)} %bitcast.30, bf16[96,2048]{1,0:T(8,128)(2,1)S(1)} %bitcast.31, ...), custom_call_target="tpu_custom_call" | custom-call | tf_op jit(solution)/shard_map/experts/pallas_call | solution.py:360
  104.4 1.0 select_bitcast_fusion
  105.5 0.6 copy.25
  (2 shorter events, 0.0 us)
Async XLA Ops:
  0.6 4.7 %copy-start = (bf16[16,128]{1,0:T(8,128)(2,1)S(1)}, bf16[16,128]{1,0:T(8,128)(2,1)}, u32[]{:S(2)}) copy-start(bf16[16,128]{1,0:T(8,128)(2,1)} %param.11) | copy-start | bytes 12292
  0.6 6.1 %copy-start.2 = (bf16[1,2048,96]{1,2,0:T(8,128)(2,1)S(1)}, bf16[1,2048,96]{1,2,0:T(8,128)(2,1)}, u32[]{:S(2)}) copy-start(bf16[1,2048,96]{1,2,0:T(8,128)(2,1)} %param.17) | copy-start | bytes 1179652
  0.7 6.1 %copy-start.1 = (bf16[1,2048,96]{1,2,0:T(8,128)(2,1)S(1)}, bf16[1,2048,96]{1,2,0:T(8,128)(2,1)}, u32[]{:S(2)}) copy-start(bf16[1,2048,96]{1,2,0:T(8,128)(2,1)} %param.16) | copy-start | bytes 1179652
  6.7 1.0 copy-start.3
  7.7 1.0 copy-start.4
  8.7 1.0 copy-start.5
  9.7 1.0 copy-start.6

commit v3 on v2

v3 whole, which is shorter than its diff:
```python
import functools

import jax
import jax.numpy as jnp
from jax import lax
from jax.experimental import pallas as pl
from jax.experimental.pallas import tpu as pltpu
from jax.sharding import PartitionSpec as P

MOMENT_DECAY = 0.9
CAPACITY = 4
LANES = 128
SIDE = 4
MESH = pl.DeviceIdType.MESH
NT = (((1,), (1,)), ((), ()))
NN = (((1,), (0,)), ((), ()))
TN = (((0,), (0,)), ((), ()))


def dot(a, b, dims):
    return lax.dot_general(a, b, dims, preferred_element_type=jnp.float32)


def kernel(
    ids_ref,
    probs_ref,
    tokens_ref,
    cot_ref,
    relocate_ref,
    wg_ref,
    wu_ref,
    wd_ref,
    mg_ref,
    mu_ref,
    md_ref,
    tok_ref,
    flag_ref,
    own_ref,
    got_ref,
    ids,
    probs,
    toks,
    cots,
    moved,
    send,
    collect,
    own,
    w,
    m,
    g,
    acc,
    sides,
    p,
    buf_a,
    buf_b,
    buf_c,
    buf_d,
    tmp_r,
    tmp_l,
    q,
    y_a,
    y_b,
    y_c,
    y_d,
    y_r,
    y_l,
    back,
    ret,
    load_sem,
    a2a_sem,
    gs_sem,
    gr_sem,
    ps_sem,
    pr_sem,
    ms_sem,
    mr_sem,
    ret_sem,
    own_sem,
):
    count = send.shape[0]
    units = wg_ref.shape[0]
    tok_rows = tokens_ref.shape[0]
    wide = count * 2 * CAPACITY
    rows = count * CAPACITY
    half = count // 2
    e = lax.axis_index("expert")
    hid = lax.axis_index("hidden")
    x, y = lax.div(hid, SIDE), lax.rem(hid, SIDE)

    def h_at(dx, dy):
        return lax.rem(x + dx, SIDE) * SIDE + lax.rem(y + dy, SIDE)

    def peer(de, dx, dy):
        return (lax.rem(e + de, count), h_at(dx, dy))

    x_right, x_left = peer(0, 1, 0), peer(0, 3, 0)
    y_right, y_left = peer(0, 0, 1), peer(0, 0, 3)
    partner = peer(half, 0, 0)

    small = [
        pltpu.make_async_copy(src, dst, load_sem.at[6 + i])
        for i, (src, dst) in enumerate(
            (
                (ids_ref, ids),
                (probs_ref, probs),
                (tokens_ref, toks),
                (cot_ref, cots),
                (relocate_ref, moved),
            )
        )
    ]
    for load in small:
        load.start()
    loads = [
        pltpu.make_async_copy(src, dst.at[pl.ds(i * units, units)], load_sem.at[j * 3 + i])
        for j, (dst, group) in enumerate(
            ((w, (wg_ref, wu_ref, wd_ref)), (m, (mg_ref, mu_ref, md_ref)))
        )
        for i, src in enumerate(group)
    ]
    for load in loads:
        load.start()

    barrier = pltpu.get_barrier_semaphore()

    def greet(i, carry):
        pl.semaphore_signal(barrier, inc=1, device_id=peer(i, 0, 0), device_id_type=MESH)
        return carry

    lax.fori_loop(1, count, greet, 0)
    for near in (x_right, x_left, y_right, y_left):
        pl.semaphore_signal(barrier, inc=1, device_id=near, device_id_type=MESH)

    for load in small:
        load.wait()
    f32, bf16 = jnp.float32, jnp.bfloat16
    slot = lax.broadcasted_iota(jnp.int32, (wide, tok_rows), 0)
    expert = slot // (2 * CAPACITY)
    place = jnp.bitwise_and(slot, 2 * CAPACITY - 1)
    named = jnp.zeros((wide, tok_rows), f32)
    scale = jnp.zeros((wide, tok_rows), f32)
    for k in range(ids_ref.shape[0]):
        hit = expert == ids[k : k + 1, :]
        named += jnp.where(hit, 1.0, 0.0)
        scale += jnp.where(hit, probs[k : k + 1, :], 0.0)
    earlier = lax.broadcasted_iota(jnp.int32, (tok_rows, tok_rows), 0)
    later = lax.broadcasted_iota(jnp.int32, (tok_rows, tok_rows), 1)
    before = jnp.where(earlier < later, 1.0, 0.0).astype(bf16)
    rank = dot(named.astype(bf16), before, NN)
    want = jnp.bitwise_and(place, CAPACITY - 1).astype(f32)
    chosen = jnp.where(rank == want, named, 0.0)
    take_x = jnp.where(place < CAPACITY, chosen, 0.0).astype(bf16)
    scale = jnp.where(place < CAPACITY, 0.0, chosen * scale)
    collect[...] = take_x
    dealing = dot(take_x, toks[...], NN)
    for _ in range(3):
        part = scale.astype(bf16)
        dealing += dot(part, cots[...], NN)
        scale = scale - part.astype(f32)
    send[...] = dealing.astype(bf16).reshape(send.shape)
    lanes = lax.broadcasted_iota(jnp.int32, moved.shape, 1)
    flag = jnp.sum(jnp.where(lanes == e, moved[...], 0), axis=1, keepdims=True)
    flag_ref[...] = jnp.broadcast_to(flag.astype(f32), flag_ref.shape)
    pl.semaphore_wait(barrier, count - 1 + 4)

    def remote(src, dst, ssem, rsem, to):
        return pltpu.make_async_remote_copy(
            src_ref=src,
            dst_ref=dst,
            send_sem=ssem,
            recv_sem=rsem,
            device_id=to,
            device_id_type=MESH,
        )

    me = h_at(0, 0)

    def deal(n):
        def step(i, carry):
            to = peer(i, 0, 0)
            remote(send.at[to[0]], g.at[me, i], a2a_sem.at[0], a2a_sem.at[n], to).start()
            return carry

        return step

    lax.fori_loop(1, half, deal(1), 0)
    lax.fori_loop(half, count, deal(2), 0)
    keep = pltpu.make_async_copy(send.at[e], g.at[me, 0], a2a_sem.at[3])
    keep.start()

    def dealt(first, size, n):
        span = pl.ds(first, size)
        return remote(send.at[span], g.at[me, span], a2a_sem.at[0], a2a_sem.at[n], x_right)

    sent = []

    def push(src, dst, sems, n, to):
        copy = remote(src, dst, sems[0].at[n], sems[1].at[n], to)
        copy.start()
        sent.append(copy)
        return copy

    gs = (gs_sem, gr_sem)

    fold = half // 2

    def part(h, c):
        return g.at[h, pl.ds(c * half, half)]

    def low(h, c):
        return g.at[h, pl.ds(c * half, fold)]

    def high(h, c):
        return g.at[h, pl.ds(c * half + fold, fold)]

    def both(pick, h, c, n, right, left):
        src = pick(h, c)
        return push(src, src, gs, 20 * c + n, right), push(src, src, gs, 20 * c + n + 1, left)

    def x_out(n, dy, c):
        return both(part, h_at(0, dy), c, 4 + 4 * n, x_right, x_left)

    def forward(n, c, left_h, right_h, arrivals, right, left):
        arrivals[0].wait_recv()
        a = low(left_h, c)
        a = push(a, a, gs, 20 * c + n, right)
        arrivals[1].wait_recv()
        b = high(right_h, c)
        return a, push(b, b, gs, 20 * c + n + 1, left)

    def x_forward(n, dy, c, arrivals):
        return forward(6 + 4 * n, c, h_at(3, dy), h_at(1, dy), arrivals, x_right, x_left)

    def absorb(dx, dy, c, first=False):
        h = h_at(dx, dy)
        cols = pl.ds(pl.multiple_of(h * LANES, LANES), LANES)
        mine = pl.ds(c * (wide // 2), wide // 2)
        term = dot(w[:, cols], part(h, c)[...].reshape(wide // 2, LANES), NT)
        if first:
            acc[:, mine] = term
        else:
            acc[:, mine] += term

    streams = (0, 1)
    y_in, x_in, x_fwd, opp = {}, {}, {}, {}

    def begin(c):
        y_in[c] = both(part, me, c, 0, y_right, y_left)
        x_in[c, 0] = x_out(0, 0, c)

    keep.wait()
    dealt(1, half - 1, 1).wait_recv()
    begin(0)
    for load in loads[:3]:
        load.wait()
    absorb(0, 0, 0, True)
    dealt(half, half, 2).wait_recv()
    begin(1)
    absorb(0, 0, 1, True)
    for c in streams:
        opp[c] = forward(2, c, h_at(0, 3), h_at(0, 1), y_in[c], y_right, y_left)
        x_in[c, 3] = x_out(1, 3, c)
        x_in[c, 1] = x_out(2, 1, c)
        x_fwd[c, 0] = x_forward(0, 0, c, x_in[c, 0])
        absorb(0, 3, c)
        absorb(0, 1, c)
    for c in streams:
        for copy in opp[c]:
            copy.wait_recv()
        x_in[c, 2] = x_out(3, 2, c)
        absorb(3, 0, c)
        absorb(1, 0, c)
        x_fwd[c, 3] = x_forward(1, 3, c, x_in[c, 3])
        absorb(3, 3, c)
        absorb(1, 3, c)
        x_fwd[c, 1] = x_forward(2, 1, c, x_in[c, 1])
        absorb(0, 2, c)
        absorb(3, 1, c)
        absorb(1, 1, c)

    def finish(c, dy):
        for copy in x_fwd[c, dy]:
            copy.wait_recv()
        absorb(2, dy, c)

    for c in streams:
        finish(c, 0)
        finish(c, 3)
        x_fwd[c, 2] = x_forward(3, 2, c, x_in[c, 2])
        absorb(3, 2, c)
        absorb(1, 2, c)
    for c in streams:
        finish(c, 1)
        finish(c, 2)

    gate = acc[pl.ds(0, units), :]
    up = acc[pl.ds(units, units), :]
    down = pltpu.roll(acc[pl.ds(2 * units, units), :], wide - CAPACITY, 1)
    lane = lax.broadcasted_iota(jnp.int32, (units, wide), 1)
    is_x = jnp.bitwise_and(lane, 2 * CAPACITY - 1) < CAPACITY
    sig = jax.nn.sigmoid(gate)
    act = gate * sig
    d_gate = down * up * sig * (1.0 + gate * (1.0 - sig))
    d_up = down * act
    hidden = pltpu.roll(jnp.where(is_x, act * up, 0.0), CAPACITY, 1)
    sides[pl.ds(0, units), :] = jnp.where(is_x, d_gate, 0.0).astype(jnp.bfloat16)
    sides[pl.ds(units, units), :] = jnp.where(is_x, d_up, 0.0).astype(jnp.bfloat16)
    sides[pl.ds(2 * units, units), :] = hidden.astype(jnp.bfloat16)

    row = lax.broadcasted_iota(jnp.int32, (rows, wide), 0)
    col = lax.broadcasted_iota(jnp.int32, (rows, wide), 1)
    slot = (row // CAPACITY) * (2 * CAPACITY) + jnp.bitwise_and(row, CAPACITY - 1)
    compact = (slot == col).astype(jnp.float32).astype(jnp.bfloat16)
    d_rows = dot(compact, sides[pl.ds(0, 2 * units), :], NT).astype(jnp.bfloat16)

    def quarter(dx):
        block = lax.rem(x + dx, SIDE)
        cols = pl.ds(pl.multiple_of(block * (SIDE * LANES), LANES), SIDE * LANES)
        value = dot(d_rows, w[pl.ds(0, 2 * units), cols], NN).astype(jnp.bfloat16)
        for j in range(SIDE):
            p[block * SIDE + j] = value[:, j * LANES : (j + 1) * LANES]
        return block * SIDE

    for load in loads[3:]:
        load.wait()
    swaps, kept = [], []

    def fresh(i):
        span = pl.ds(i * units, units)
        for k in range(SIDE * SIDE // 2):
            rhs = jnp.concatenate(
                [g[2 * k].reshape(wide, LANES), g[2 * k + 1].reshape(wide, LANES)], axis=1
            )
            grad = dot(sides[span, :], rhs, NN)
            cols = pl.ds(2 * k * LANES, 2 * LANES)
            old = m[span, cols].astype(jnp.float32)
            own[span, cols] = (MOMENT_DECAY * old + (1.0 - MOMENT_DECAY) * grad).astype(
                jnp.bfloat16
            )
        copy = pltpu.make_async_copy(own.at[span], own_ref.at[span], own_sem.at[i])
        copy.start()
        kept.append(copy)

    def swap(i):
        span = pl.ds(i * (units // 2), units // 2)
        swaps.append(push(own.at[span], got_ref.at[span], (ms_sem, mr_sem), i, partner))

    ps = (ps_sem, pr_sem)
    o = quarter(2)
    from_a = push(p.at[pl.ds(o, 2)], buf_a, ps, 0, x_right)
    from_b = push(p.at[pl.ds(o + 2, 2)], buf_b, ps, 1, x_left)
    fresh(0)
    swap(0)
    swap(1)
    r = quarter(1)
    c_high = push(p.at[pl.ds(r + 2, 2)], buf_c.at[pl.ds(2, 2)], ps, 2, x_right)
    l = quarter(3)
    d_low = push(p.at[pl.ds(l, 2)], buf_d.at[pl.ds(0, 2)], ps, 3, x_left)
    fresh(1)
    swap(2)
    s = quarter(0)

    def add(a, b):
        return (a.astype(jnp.float32) + b.astype(jnp.float32)).astype(jnp.bfloat16)

    from_a.wait_recv()
    tmp_r[...] = add(p[pl.ds(r, 2)], buf_a[...])
    c_low = push(tmp_r, buf_c.at[pl.ds(0, 2)], ps, 4, x_right)
    from_b.wait_recv()
    tmp_l[...] = add(p[pl.ds(l + 2, 2)], buf_b[...])
    d_high = push(tmp_l, buf_d.at[pl.ds(2, 2)], ps, 5, x_left)
    for copy in (c_high, d_low, c_low, d_high):
        copy.wait_recv()
    q[...] = (
        p[pl.ds(s, SIDE)].astype(f32) + buf_c[...].astype(f32) + buf_d[...].astype(f32)
    ).astype(jnp.bfloat16)

    top, low_rows = pl.ds(0, rows // 2), pl.ds(rows // 2, rows // 2)
    yo, yr, yl = lax.rem(y + 2, SIDE), lax.rem(y + 1, SIDE), lax.rem(y + 3, SIDE)
    from_a = push(q.at[yo, top], y_a, ps, 6, y_right)
    from_b = push(q.at[yo, low_rows], y_b, ps, 7, y_left)
    c_high = push(q.at[yr, low_rows], y_c.at[low_rows], ps, 8, y_right)
    d_low = push(q.at[yl, top], y_d.at[top], ps, 9, y_left)
    swap(3)
    fresh(2)
    from_a.wait_recv()
    y_r[...] = add(q[yr, top], y_a[...])
    c_low = push(y_r, y_c.at[top], ps, 10, y_right)
    from_b.wait_recv()
    y_l[...] = add(q[yl, low_rows], y_b[...])
    d_high = push(y_l, y_d.at[low_rows], ps, 11, y_left)
    swap(4)
    for copy in (c_high, d_low, c_low, d_high):
        copy.wait_recv()
    total = (q[y].astype(f32) + y_c[...].astype(f32) + y_d[...].astype(f32)).astype(jnp.bfloat16)

    row = lax.broadcasted_iota(jnp.int32, (wide, rows), 0)
    col = lax.broadcasted_iota(jnp.int32, (wide, rows), 1)
    slot = (col // CAPACITY) * (2 * CAPACITY) + jnp.bitwise_and(col, CAPACITY - 1)
    spread = (slot == row).astype(jnp.float32).astype(jnp.bfloat16)
    back[...] = dot(spread, total, NN).astype(jnp.bfloat16).reshape(back.shape)

    def give(i, carry):
        to = peer(count - i, 0, 0)
        remote(back.at[i], ret.at[e], ret_sem.at[0], ret_sem.at[1], to).start()
        return carry

    lax.fori_loop(1, count, give, 0)
    swap(5)
    keep = pltpu.make_async_copy(back.at[0], ret.at[e], ret_sem.at[2])
    keep.start()
    keep.wait()
    given = remote(
        back.at[pl.ds(0, count - 1)],
        ret.at[pl.ds(0, count - 1)],
        ret_sem.at[0],
        ret_sem.at[1],
        x_right,
    )
    given.wait_recv()
    tok_ref[...] = dot(collect[...], ret[...].reshape(wide, LANES), TN).astype(jnp.bfloat16)

    for copy in swaps:
        copy.wait_recv()
    for copy in sent:
        copy.wait_send()
    dealt(1, count - 1, 1).wait_send()
    given.wait_send()
    for copy in kept:
        copy.wait()


def run_kernel(small, weights, moments):
    ids, _, tokens, _, relocate = small
    count = relocate.shape[1]
    tok_rows = tokens.shape[0]
    units, width = weights[0].shape
    wide, rows = count * 2 * CAPACITY, count * CAPACITY
    blocks = SIDE * SIDE
    bf16, f32 = jnp.bfloat16, jnp.float32
    vmem, dma = pltpu.VMEM, pltpu.SemaphoreType.DMA
    return pl.pallas_call(
        kernel,
        out_shape=(
            jax.ShapeDtypeStruct((tok_rows, LANES), bf16),
            jax.ShapeDtypeStruct((1, width), f32),
            jax.ShapeDtypeStruct((3 * units, width), bf16),
            jax.ShapeDtypeStruct((3 * units, width), bf16),
        ),
        in_specs=[pl.BlockSpec(memory_space=pl.ANY)] * 11,
        out_specs=(
            pl.BlockSpec(memory_space=vmem),
            pl.BlockSpec(memory_space=vmem),
            pl.BlockSpec(memory_space=pl.ANY),
            pl.BlockSpec(memory_space=pl.ANY),
        ),
        scratch_shapes=[
            vmem(ids.shape, jnp.int32),
            vmem(ids.shape, f32),
            vmem(tokens.shape, bf16),
            vmem(tokens.shape, bf16),
            vmem(relocate.shape, jnp.int32),
            vmem((count, 2 * CAPACITY, LANES), bf16),
            vmem((wide, tok_rows), bf16),
            vmem((3 * units, width), bf16),
            vmem((3 * units, width), bf16),
            vmem((3 * units, width), bf16),
            vmem((blocks, count, 2 * CAPACITY, LANES), bf16),
            vmem((3 * units, wide), f32),
            vmem((3 * units, wide), bf16),
            vmem((blocks, rows, LANES), bf16),
            vmem((2, rows, LANES), bf16),
            vmem((2, rows, LANES), bf16),
            vmem((4, rows, LANES), bf16),
            vmem((4, rows, LANES), bf16),
            vmem((2, rows, LANES), bf16),
            vmem((2, rows, LANES), bf16),
            vmem((4, rows, LANES), bf16),
            vmem((rows // 2, LANES), bf16),
            vmem((rows // 2, LANES), bf16),
            vmem((rows, LANES), bf16),
            vmem((rows, LANES), bf16),
            vmem((rows // 2, LANES), bf16),
            vmem((rows // 2, LANES), bf16),
            vmem((count, 2 * CAPACITY, LANES), bf16),
            vmem((count, 2 * CAPACITY, LANES), bf16),
            dma((11,)),
            dma((4,)),
            dma((40,)),
            dma((40,)),
            dma((12,)),
            dma((12,)),
            dma((6,)),
            dma((6,)),
            dma((3,)),
            dma((3,)),
        ],
        compiler_params=pltpu.CompilerParams(
            collective_id=0, has_side_effects=True, vmem_limit_bytes=67043328
        ),
        name="experts",
    )(*small, *weights, *moments)


def on_device(
    tokens,
    out_cotangent,
    expert_ids,
    gate_probs,
    relocate,
    w_gate,
    w_up,
    w_down,
    moment_gate,
    moment_up,
    moment_down,
):
    token_grad, flag, own, got = run_kernel(
        (expert_ids.T, gate_probs.T, tokens, out_cotangent, relocate[None]),
        (w_gate[0].T, w_up[0].T, w_down[0]),
        (moment_gate[0].T, moment_up[0].T, moment_down[0]),
    )
    units = w_down.shape[1]
    fresh = [
        jnp.where(flag == 1.0, got[i * units : (i + 1) * units], own[i * units : (i + 1) * units])
        for i in range(3)
    ]
    return (token_grad, fresh[0].T[None], fresh[1].T[None], fresh[2][None])


def solution(mesh):
    return jax.shard_map(
        on_device,
        mesh=mesh,
        in_specs=(
            P("expert", "hidden"),
            P("expert", "hidden"),
            P("expert", None),
            P("expert", None),
            P(),
            P("expert", None, "hidden"),
            P("expert", None, "hidden"),
            P("expert", "hidden", None),
            P("expert", None, "hidden"),
            P("expert", None, "hidden"),
            P("expert", "hidden", None),
        ),
        out_specs=(
            P("expert", "hidden"),
            P("expert", None, "hidden"),
            P("expert", None, "hidden"),
            P("expert", "hidden", None),
        ),
        check_vma=False,
    )
```

time: 108 us -> 100 us (0.926); the launches traced: 106 us -> 99.9 us
  local copies, waits for them, and re-layouts: 6.27 us -> 0.6 us
  Pallas kernels: 93.7 us -> 95.2 us
  matrix products: 1.33 us -> 0 us
    unnamed x17 -> x3, local copies, waits for them, and re-layouts: 6.11 us -> 0.6 us
    reduce_sum x3 -> x0, other arithmetic: 1.7 us -> none  [the longest x1 1.36 us: on_device(): swapping = jnp.sum(jnp.where(experts_iota == my_slot, relocate, 0)) == 1]
    broadcast_in_dim x1, other arithmetic: 1.05 us -> 2.64 us  [on_device(): return (token_grad, fresh[0].T[None], fresh[1].T[None], fresh[2][None])]
    pallas_call x1, Pallas kernels: 93.7 us -> 95.2 us  [run_kernel(): pl.pallas_call(kernel, out_shape=(jax.ShapeDtypeStruct((tok_rows, LANES),...]
    dot_general x2 -> x0, matrix products: 1.33 us -> none  [the longest x1 1.09 us: on_device(): jnp.dot(weighted, out_cotangent.astype(jnp.float32), precision=lax.Precis...]
where the time goes in v3:
time: 100 us; the launch traced here: 99.9 us
  Pallas kernels  95.2 us (95%)
  other arithmetic  3.37 us (3%)
    pallas_call x1, Pallas kernels, run_kernel(): pl.pallas_call(kernel, out_shape=(jax.ShapeDtypeStruct((tok_rows, LANES),...  95.2 us
    broadcast_in_dim x1, other arithmetic, on_device(): return (token_grad, fresh[0].T[None], fresh[1].T[None], fresh[2][None])  2.64 us

profile of v3, /device:TPU:1, one launch (start us, length us, event | category | flops | bytes accessed | tf_op | source)
XLA Modules:
  0.0 99.9 jit_solution(11161875428194076850)
XLA Ops:
  0.6 95.2 %experts.1 = (bf16[16,128]{1,0:T(8,128)(2,1)}, f32[1,2048]{1,0:T(1,128)}, bf16[288,2048]{1,0:T(8,128)(2,1)}, bf16[288,2048]{1,0:T(8,128)(2,1)}) custom-call(s32[8,16]{1,0:T(8,128)} %bitcast.33, f32[8,16]{1,0:T(8,128)} %bitcast.34, bf16[16,128]{1,0:T(8,128)(2,1)} %tokens_ref.1, bf16[16,128]{1,0:T(8,128)(2,1)} %cot_ref.1, s32[1,64]{1,0:T(1,128)} %bitcast.35, ...), custom_call_target="tpu_custom_call" | custom-call | tf_op jit(solution)/shard_map/experts/pallas_call | solution.py:442
  95.9 0.7 compare_reduce_fusion
  96.6 0.0 copy-start
  96.6 2.6 %select_bitcast_fusion = (bf16[1,96,2048]{2,1,0:T(8,128)(2,1)}, bf16[1,2048,96]{1,2,0:T(8,128)(2,1)}, bf16[1,2048,96]{1,2,0:T(8,128)(2,1)}) fusion(bf16[288,2048]{1,0:T(8,128)(2,1)} %get-tuple-element.11, bf16[288,2048]{1,0:T(8,128)(2,1)} %get-tuple-element.10, pred[2048]{0:T(1024)(128)(4,1)S(1)} %compare_reduce_fusion), kind=kLoop, calls=%fused_computation | loop fusion | flops 589824 | bytes 3540992 | tf_op jit(solution)/shard_map/broadcast_in_dim | solution.py:528
  99.3 0.0 copy-done
  99.3 0.6 copy.16
Async XLA Ops:
  96.6 2.7 %copy-start = (bf16[16,128]{1,0:T(8,128)(2,1)S(1)}, bf16[16,128]{1,0:T(8,128)(2,1)}, u32[]{:S(2)}) copy-start(bf16[16,128]{1,0:T(8,128)(2,1)} %get-tuple-element.19) | copy-start | bytes 12292

commit v4 on v3

--- a/solution.py
+++ b/solution.py
@@ -34,9 +34,9 @@
     mu_ref,
     md_ref,
     tok_ref,
-    flag_ref,
-    own_ref,
-    got_ref,
+    new_gate_ref,
+    new_up_ref,
+    new_down_ref,
     ids,
     probs,
     toks,
@@ -45,6 +45,8 @@
     send,
     collect,
     own,
+    got,
+    new,
     w,
     m,
     g,
@@ -123,11 +125,22 @@
 
     barrier = pltpu.get_barrier_semaphore()
 
-    def greet(i, carry):
+    def far_first(act):
+        def near(k, carry):
+            act(half // 2 + lax.div(k + 1, 2) * (1 - 2 * lax.rem(k, 2)))
+            return carry
+
+        def across(k, carry):
+            act(half + half // 2 + lax.div(k + 1, 2) * (1 - 2 * lax.rem(k, 2)))
+            return carry
+
+        lax.fori_loop(0, half - 1, near, 0)
+        lax.fori_loop(0, half, across, 0)
+
+    def greet(i):
         pl.semaphore_signal(barrier, inc=1, device_id=peer(i, 0, 0), device_id_type=MESH)
-        return carry
-
-    lax.fori_loop(1, count, greet, 0)
+
+    far_first(greet)
     for near in (x_right, x_left, y_right, y_left):
         pl.semaphore_signal(barrier, inc=1, device_id=near, device_id_type=MESH)
 
@@ -160,7 +173,6 @@
     send[...] = dealing.astype(bf16).reshape(send.shape)
     lanes = lax.broadcasted_iota(jnp.int32, moved.shape, 1)
     flag = jnp.sum(jnp.where(lanes == e, moved[...], 0), axis=1, keepdims=True)
-    flag_ref[...] = jnp.broadcast_to(flag.astype(f32), flag_ref.shape)
     pl.semaphore_wait(barrier, count - 1 + 4)
 
     def remote(src, dst, ssem, rsem, to):
@@ -175,17 +187,18 @@
 
     me = h_at(0, 0)
 
-    def deal(n):
-        def step(i, carry):
-            to = peer(i, 0, 0)
-            remote(send.at[to[0]], g.at[me, i], a2a_sem.at[0], a2a_sem.at[n], to).start()
-            return carry
-
-        return step
-
-    lax.fori_loop(1, half, deal(1), 0)
-    lax.fori_loop(half, count, deal(2), 0)
-    keep = pltpu.make_async_copy(send.at[e], g.at[me, 0], a2a_sem.at[3])
+    quart = half // 2
+    sizes = (half, quart, quart)
+    starts = (0, half, half + quart)
+    streams = (0, 1, 2)
+
+    def deal(i):
+        to = peer(i, 0, 0)
+        n = 1 + lax.div(i, half) + lax.div(i, half + quart)
+        remote(send.at[to[0]], g.at[me, i], a2a_sem.at[0], a2a_sem.at[n], to).start()
+
+    far_first(deal)
+    keep = pltpu.make_async_copy(send.at[e], g.at[me, 0], a2a_sem.at[4])
     keep.start()
 
     def dealt(first, size, n):
@@ -202,51 +215,62 @@
 
     gs = (gs_sem, gr_sem)
 
-    fold = half // 2
+    def block(c, second, first):
+        return h_at(second, first) if c < 2 else h_at(first, second)
+
+    def sides_of(c, stage):
+        return (y_right, y_left) if (stage == 0) == (c < 2) else (x_right, x_left)
 
     def part(h, c):
-        return g.at[h, pl.ds(c * half, half)]
+        return g.at[h, pl.ds(starts[c], sizes[c])]
 
     def low(h, c):
-        return g.at[h, pl.ds(c * half, fold)]
+        return g.at[h, pl.ds(starts[c], sizes[c] // 2)]
 
     def high(h, c):
-        return g.at[h, pl.ds(c * half + fold, fold)]
-
-    def both(pick, h, c, n, right, left):
-        src = pick(h, c)
-        return push(src, src, gs, 20 * c + n, right), push(src, src, gs, 20 * c + n + 1, left)
-
-    def x_out(n, dy, c):
-        return both(part, h_at(0, dy), c, 4 + 4 * n, x_right, x_left)
-
-    def forward(n, c, left_h, right_h, arrivals, right, left):
+        return g.at[h, pl.ds(starts[c] + sizes[c] // 2, sizes[c] // 2)]
+
+    def out(n, h, c, stage):
+        src = part(h, c)
+        right, left = sides_of(c, stage)
+        n = 20 * c + n
+        return push(src, src, gs, n, right), push(src, src, gs, n + 1, left)
+
+    def forward(n, c, left_h, right_h, arrivals, stage):
+        right, left = sides_of(c, stage)
+        n = 20 * c + n
         arrivals[0].wait_recv()
         a = low(left_h, c)
-        a = push(a, a, gs, 20 * c + n, right)
+        a = push(a, a, gs, n, right)
         arrivals[1].wait_recv()
         b = high(right_h, c)
-        return a, push(b, b, gs, 20 * c + n + 1, left)
-
-    def x_forward(n, dy, c, arrivals):
-        return forward(6 + 4 * n, c, h_at(3, dy), h_at(1, dy), arrivals, x_right, x_left)
-
-    def absorb(dx, dy, c, first=False):
-        h = h_at(dx, dy)
+        return a, push(b, b, gs, n + 1, left)
+
+    order = (0, 3, 1, 2)
+
+    def second_out(b, c):
+        return out(4 + 4 * order.index(b), block(c, 0, b), c, 1)
+
+    def second_forward(b, c):
+        n = 6 + 4 * order.index(b)
+        fwd[c, b] = forward(n, c, block(c, 3, b), block(c, 1, b), into[c, b], 1)
+
+    def absorb(a, b, c, begins=False):
+        h = block(c, a, b)
         cols = pl.ds(pl.multiple_of(h * LANES, LANES), LANES)
-        mine = pl.ds(c * (wide // 2), wide // 2)
-        term = dot(w[:, cols], part(h, c)[...].reshape(wide // 2, LANES), NT)
-        if first:
+        wide_c = sizes[c] * 2 * CAPACITY
+        mine = pl.ds(starts[c] * 2 * CAPACITY, wide_c)
+        term = dot(w[:, cols], part(h, c)[...].reshape(wide_c, LANES), NT)
+        if begins:
             acc[:, mine] = term
         else:
             acc[:, mine] += term
 
-    streams = (0, 1)
-    y_in, x_in, x_fwd, opp = {}, {}, {}, {}
+    first_in, into, fwd, opp = {}, {}, {}, {}
 
     def begin(c):
-        y_in[c] = both(part, me, c, 0, y_right, y_left)
-        x_in[c, 0] = x_out(0, 0, c)
+        first_in[c] = out(0, me, c, 0)
+        into[c, 0] = second_out(0, c)
 
     keep.wait()
     dealt(1, half - 1, 1).wait_recv()
@@ -254,44 +278,48 @@
     for load in loads[:3]:
         load.wait()
     absorb(0, 0, 0, True)
-    dealt(half, half, 2).wait_recv()
-    begin(1)
-    absorb(0, 0, 1, True)
+    for c in (1, 2):
+        dealt(starts[c], sizes[c], c + 1).wait_recv()
+        begin(c)
+    for c in (1, 2):
+        absorb(0, 0, c, True)
     for c in streams:
-        opp[c] = forward(2, c, h_at(0, 3), h_at(0, 1), y_in[c], y_right, y_left)
-        x_in[c, 3] = x_out(1, 3, c)
-        x_in[c, 1] = x_out(2, 1, c)
-        x_fwd[c, 0] = x_forward(0, 0, c, x_in[c, 0])
+        opp[c] = forward(2, c, block(c, 0, 3), block(c, 0, 1), first_in[c], 0)
+        into[c, 3] = second_out(3, c)
+        into[c, 1] = second_out(1, c)
+        second_forward(0, c)
+    for c in streams:
         absorb(0, 3, c)
         absorb(0, 1, c)
+        absorb(3, 0, c)
+        absorb(1, 0, c)
     for c in streams:
         for copy in opp[c]:
             copy.wait_recv()
-        x_in[c, 2] = x_out(3, 2, c)
-        absorb(3, 0, c)
-        absorb(1, 0, c)
-        x_fwd[c, 3] = x_forward(1, 3, c, x_in[c, 3])
+        into[c, 2] = second_out(2, c)
+        second_forward(3, c)
+    for c in streams:
+        absorb(0, 2, c)
         absorb(3, 3, c)
         absorb(1, 3, c)
-        x_fwd[c, 1] = x_forward(2, 1, c, x_in[c, 1])
-        absorb(0, 2, c)
+
+    def finish(c, b):
+        for copy in fwd[c, b]:
+            copy.wait_recv()
+        absorb(2, b, c)
+
+    for c in streams:
+        second_forward(1, c)
         absorb(3, 1, c)
         absorb(1, 1, c)
-
-    def finish(c, dy):
-        for copy in x_fwd[c, dy]:
-            copy.wait_recv()
-        absorb(2, dy, c)
-
     for c in streams:
         finish(c, 0)
-        finish(c, 3)
-        x_fwd[c, 2] = x_forward(3, 2, c, x_in[c, 2])
+        second_forward(2, c)
         absorb(3, 2, c)
         absorb(1, 2, c)
-    for c in streams:
-        finish(c, 1)
-        finish(c, 2)
+    for b in (3, 1, 2):
+        for c in streams:
+            finish(c, b)
 
     gate = acc[pl.ds(0, units), :]
     up = acc[pl.ds(units, units), :]
@@ -323,7 +351,7 @@
 
     for load in loads[3:]:
         load.wait()
-    swaps, kept = [], []
+    swaps, kept = {}, []
 
     def fresh(i):
         span = pl.ds(i * units, units)
@@ -337,13 +365,24 @@
             own[span, cols] = (MOMENT_DECAY * old + (1.0 - MOMENT_DECAY) * grad).astype(
                 jnp.bfloat16
             )
-        copy = pltpu.make_async_copy(own.at[span], own_ref.at[span], own_sem.at[i])
+
+    def swap(i):
+        span = pl.ds(i * (units // 2), units // 2)
+        swaps[i] = push(own.at[span], got.at[span], (ms_sem, mr_sem), i, partner)
+
+    def land(i):
+        for j in (2 * i, 2 * i + 1):
+            swaps[j].wait_recv()
+            span = pl.ds(j * (units // 2), units // 2)
+            moves = jnp.broadcast_to(flag, (units // 2, got.shape[1])) == 1
+            new[span, :] = jnp.where(
+                moves, got[span, :].astype(f32), own[span, :].astype(f32)
+            ).astype(bf16)
+        span = pl.ds(i * units, units)
+        target = (new_gate_ref, new_up_ref, new_down_ref)[i]
+        copy = pltpu.make_async_copy(new.at[span], target, own_sem.at[i])
         copy.start()
         kept.append(copy)
-
-    def swap(i):
-        span = pl.ds(i * (units // 2), units // 2)
-        swaps.append(push(own.at[span], got_ref.at[span], (ms_sem, mr_sem), i, partner))
 
     ps = (ps_sem, pr_sem)
     o = quarter(2)
@@ -400,12 +439,11 @@
     spread = (slot == row).astype(jnp.float32).astype(jnp.bfloat16)
     back[...] = dot(spread, total, NN).astype(jnp.bfloat16).reshape(back.shape)
 
-    def give(i, carry):
+    def give(i):
         to = peer(count - i, 0, 0)
         remote(back.at[i], ret.at[e], ret_sem.at[0], ret_sem.at[1], to).start()
-        return carry
-
-    lax.fori_loop(1, count, give, 0)
+
+    far_first(give)
     swap(5)
     keep = pltpu.make_async_copy(back.at[0], ret.at[e], ret_sem.at[2])
     keep.start()
@@ -417,11 +455,12 @@
         ret_sem.at[1],
         x_right,
     )
+    land(0)
     given.wait_recv()
     tok_ref[...] = dot(collect[...], ret[...].reshape(wide, LANES), TN).astype(jnp.bfloat16)
 
-    for copy in swaps:
-        copy.wait_recv()
+    land(1)
+    land(2)
     for copy in sent:
         copy.wait_send()
     dealt(1, count - 1, 1).wait_send()
@@ -443,14 +482,14 @@
         kernel,
         out_shape=(
             jax.ShapeDtypeStruct((tok_rows, LANES), bf16),
-            jax.ShapeDtypeStruct((1, width), f32),
-            jax.ShapeDtypeStruct((3 * units, width), bf16),
-            jax.ShapeDtypeStruct((3 * units, width), bf16),
+            jax.ShapeDtypeStruct((units, width), bf16),
+            jax.ShapeDtypeStruct((units, width), bf16),
+            jax.ShapeDtypeStruct((units, width), bf16),
         ),
         in_specs=[pl.BlockSpec(memory_space=pl.ANY)] * 11,
         out_specs=(
             pl.BlockSpec(memory_space=vmem),
-            pl.BlockSpec(memory_space=vmem),
+            pl.BlockSpec(memory_space=pl.ANY),
             pl.BlockSpec(memory_space=pl.ANY),
             pl.BlockSpec(memory_space=pl.ANY),
         ),
@@ -462,6 +501,8 @@
             vmem(relocate.shape, jnp.int32),
             vmem((count, 2 * CAPACITY, LANES), bf16),
             vmem((wide, tok_rows), bf16),
+            vmem((3 * units, width), bf16),
+            vmem((3 * units, width), bf16),
             vmem((3 * units, width), bf16),
             vmem((3 * units, width), bf16),
             vmem((3 * units, width), bf16),
@@ -485,9 +526,9 @@
             vmem((count, 2 * CAPACITY, LANES), bf16),
             vmem((count, 2 * CAPACITY, LANES), bf16),
             dma((11,)),
-            dma((4,)),
-            dma((40,)),
-            dma((40,)),
+            dma((5,)),
+            dma((60,)),
+            dma((60,)),
             dma((12,)),
             dma((12,)),
             dma((6,)),
@@ -515,17 +556,12 @@
     moment_up,
     moment_down,
 ):
-    token_grad, flag, own, got = run_kernel(
+    token_grad, new_gate, new_up, new_down = run_kernel(
         (expert_ids.T, gate_probs.T, tokens, out_cotangent, relocate[None]),
         (w_gate[0].T, w_up[0].T, w_down[0]),
         (moment_gate[0].T, moment_up[0].T, moment_down[0]),
     )
-    units = w_down.shape[1]
-    fresh = [
-        jnp.where(flag == 1.0, got[i * units : (i + 1) * units], own[i * units : (i + 1) * units])
-        for i in range(3)
-    ]
-    return (token_grad, fresh[0].T[None], fresh[1].T[None], fresh[2][None])
+    return (token_grad, new_gate.T[None], new_up.T[None], new_down[None])
 
 
 def solution(mesh):

time: 100 us -> 99.4 us (level)
  local copies, waits for them, and re-layouts: 0.6 us -> 4.97 us
  other arithmetic: 3.37 us -> 0 us
  Pallas kernels: 95.2 us -> 93.4 us
    unnamed x3 -> x10, local copies, waits for them, and re-layouts: 0.6 us -> 4.97 us
    broadcast_in_dim x1 -> x0, other arithmetic: 2.64 us -> none  [on_device(): return (token_grad, fresh[0].T[None], fresh[1].T[None], fresh[2][None])]
    pallas_call x1, Pallas kernels: 95.2 us -> 93.4 us  [run_kernel(): pl.pallas_call(kernel, out_shape=(jax.ShapeDtypeStruct((tok_rows, LANES),...]
where the time goes in v4:
time: 99.4 us; the launch traced here: 99.1 us
  Pallas kernels  93.4 us (94%)
  local copies, waits for them, and re-layouts  4.97 us (5%)
    pallas_call x1, Pallas kernels, run_kernel(): pl.pallas_call(kernel, out_shape=(jax.ShapeDtypeStruct((tok_rows, LANES),...  93.4 us
    unnamed x10, local copies, waits for them, and re-layouts  4.97 us

profile of v4, /device:TPU:1, one launch (start us, length us, event | category | flops | bytes accessed | tf_op | source)
XLA Modules:
  0.0 99.1 jit_solution(171690536582034473)
XLA Ops:
  0.6 93.4 %experts.1 = (bf16[16,128]{1,0:T(8,128)(2,1)}, bf16[96,2048]{1,0:T(8,128)(2,1)}, bf16[96,2048]{1,0:T(8,128)(2,1)}, bf16[96,2048]{1,0:T(8,128)(2,1)}) custom-call(s32[8,16]{1,0:T(8,128)} %bitcast.33, f32[8,16]{1,0:T(8,128)} %bitcast.34, bf16[16,128]{1,0:T(8,128)(2,1)} %tokens_ref.1, bf16[16,128]{1,0:T(8,128)(2,1)} %cot_ref.1, s32[1,64]{1,0:T(1,128)} %bitcast.35, ...), custom_call_target="tpu_custom_call" | custom-call | tf_op jit(solution)/shard_map/experts/pallas_call | solution.py:481
  94.1 0.0 copy-start.2
  94.1 0.7 copy-done.2
  94.8 0.6 copy.19
  95.4 0.0 copy-start.1
  95.4 1.8 %copy.20 = bf16[1,2048,96]{1,2,0:T(8,128)(2,1)} copy(bf16[1,2048,96]{1,2,0:T(8,128)(2,1)} %bitcast.26) | data formatting | bytes 786432
  97.2 0.0 copy-done.1
  97.2 0.0 copy-start
  97.2 0.7 copy.21
  97.9 0.4 copy-done
  98.3 0.7 copy.22
Async XLA Ops:
  94.1 0.7 copy-start.2
  95.4 1.8 %copy-start.1 = (bf16[96,2048]{1,0:T(8,128)(2,1)S(1)}, bf16[96,2048]{1,0:T(8,128)(2,1)}, u32[]{:S(2)}) copy-start(bf16[96,2048]{1,0:T(8,128)(2,1)} %get-tuple-element.10) | copy-start | bytes 1179652
  97.2 1.1 %copy-start = (bf16[96,2048]{1,0:T(8,128)(2,1)S(1)}, bf16[96,2048]{1,0:T(8,128)(2,1)}, u32[]{:S(2)}) copy-start(bf16[96,2048]{1,0:T(8,128)(2,1)} %get-tuple-element.11) | copy-start | bytes 1179652

commit v5 on v4

--- a/solution.py
+++ b/solution.py
@@ -34,9 +34,7 @@
     mu_ref,
     md_ref,
     tok_ref,
-    new_gate_ref,
-    new_up_ref,
-    new_down_ref,
+    new_ref,
     ids,
     probs,
     toks,
@@ -125,22 +123,17 @@
 
     barrier = pltpu.get_barrier_semaphore()
 
-    def far_first(act):
-        def near(k, carry):
-            act(half // 2 + lax.div(k + 1, 2) * (1 - 2 * lax.rem(k, 2)))
+    def in_order(act):
+        def step(i, carry):
+            act(i)
             return carry
 
-        def across(k, carry):
-            act(half + half // 2 + lax.div(k + 1, 2) * (1 - 2 * lax.rem(k, 2)))
-            return carry
-
-        lax.fori_loop(0, half - 1, near, 0)
-        lax.fori_loop(0, half, across, 0)
+        lax.fori_loop(1, count, step, 0)
 
     def greet(i):
         pl.semaphore_signal(barrier, inc=1, device_id=peer(i, 0, 0), device_id_type=MESH)
 
-    far_first(greet)
+    in_order(greet)
     for near in (x_right, x_left, y_right, y_left):
         pl.semaphore_signal(barrier, inc=1, device_id=near, device_id_type=MESH)
 
@@ -197,7 +190,7 @@
         n = 1 + lax.div(i, half) + lax.div(i, half + quart)
         remote(send.at[to[0]], g.at[me, i], a2a_sem.at[0], a2a_sem.at[n], to).start()
 
-    far_first(deal)
+    in_order(deal)
     keep = pltpu.make_async_copy(send.at[e], g.at[me, 0], a2a_sem.at[4])
     keep.start()
 
@@ -379,8 +372,7 @@
                 moves, got[span, :].astype(f32), own[span, :].astype(f32)
             ).astype(bf16)
         span = pl.ds(i * units, units)
-        target = (new_gate_ref, new_up_ref, new_down_ref)[i]
-        copy = pltpu.make_async_copy(new.at[span], target, own_sem.at[i])
+        copy = pltpu.make_async_copy(new.at[span], new_ref.at[span], own_sem.at[i])
         copy.start()
         kept.append(copy)
 
@@ -443,7 +435,7 @@
         to = peer(count - i, 0, 0)
         remote(back.at[i], ret.at[e], ret_sem.at[0], ret_sem.at[1], to).start()
 
-    far_first(give)
+    in_order(give)
     swap(5)
     keep = pltpu.make_async_copy(back.at[0], ret.at[e], ret_sem.at[2])
     keep.start()
@@ -482,15 +474,11 @@
         kernel,
         out_shape=(
             jax.ShapeDtypeStruct((tok_rows, LANES), bf16),
-            jax.ShapeDtypeStruct((units, width), bf16),
-            jax.ShapeDtypeStruct((units, width), bf16),
-            jax.ShapeDtypeStruct((units, width), bf16),
+            jax.ShapeDtypeStruct((3 * units, width), bf16),
         ),
         in_specs=[pl.BlockSpec(memory_space=pl.ANY)] * 11,
         out_specs=(
             pl.BlockSpec(memory_space=vmem),
-            pl.BlockSpec(memory_space=pl.ANY),
-            pl.BlockSpec(memory_space=pl.ANY),
             pl.BlockSpec(memory_space=pl.ANY),
         ),
         scratch_shapes=[
@@ -556,11 +544,13 @@
     moment_up,
     moment_down,
 ):
-    token_grad, new_gate, new_up, new_down = run_kernel(
+    token_grad, new = run_kernel(
         (expert_ids.T, gate_probs.T, tokens, out_cotangent, relocate[None]),
         (w_gate[0].T, w_up[0].T, w_down[0]),
         (moment_gate[0].T, moment_up[0].T, moment_down[0]),
     )
+    units = w_down.shape[1]
+    new_gate, new_up, new_down = (new[i * units : (i + 1) * units] for i in range(3))
     return (token_grad, new_gate.T[None], new_up.T[None], new_down[None])
 
 

time: 99.4 us -> 98.4 us (0.990)
  local copies, waits for them, and re-layouts: 4.97 us -> 2.86 us
  Pallas kernels: 93.4 us -> 94.7 us
    unnamed x10 -> x3, local copies, waits for them, and re-layouts: 4.97 us -> 0.6 us
    broadcast_in_dim x0 -> x1, local copies, waits for them, and re-layouts: none -> 2.26 us  [on_device(): return (token_grad, new_gate.T[None], new_up.T[None], new_down[None])]
    pallas_call x1, Pallas kernels: 93.4 us -> 94.7 us  [run_kernel(): pl.pallas_call(kernel, out_shape=(jax.ShapeDtypeStruct((tok_rows, LANES),...]
where the time goes in v5:
time: 98.4 us; the launch traced here: 98.2 us
  Pallas kernels  94.7 us (96%)
  local copies, waits for them, and re-layouts  2.86 us (3%)
    pallas_call x1, Pallas kernels, run_kernel(): pl.pallas_call(kernel, out_shape=(jax.ShapeDtypeStruct((tok_rows, LANES),...  94.7 us
    broadcast_in_dim x1, local copies, waits for them, and re-layouts, on_device(): return (token_grad, new_gate.T[None], new_up.T[None], new_down[None])  2.26 us

profile of v5, /device:TPU:1, one launch (start us, length us, event | category | flops | bytes accessed | tf_op | source)
XLA Modules:
  0.0 98.2 jit_solution(7256707170288755741)
XLA Ops:
  0.6 94.7 %experts.1 = (bf16[16,128]{1,0:T(8,128)(2,1)}, bf16[288,2048]{1,0:T(8,128)(2,1)}) custom-call(s32[8,16]{1,0:T(8,128)} %bitcast.33, f32[8,16]{1,0:T(8,128)} %bitcast.34, bf16[16,128]{1,0:T(8,128)(2,1)} %tokens_ref.1, bf16[16,128]{1,0:T(8,128)(2,1)} %cot_ref.1, s32[1,64]{1,0:T(1,128)} %bitcast.35, bf16[96,2048]{1,0:T(8,128)(2,1)} %bitcast.27, ...), custom_call_target="tpu_custom_call" | custom-call | tf_op jit(solution)/shard_map/experts/pallas_call | solution.py:473
  95.4 0.0 copy-start
  95.4 2.3 %slice_bitcast_fusion = (bf16[1,96,2048]{2,1,0:T(8,128)(2,1)}, bf16[1,2048,96]{1,2,0:T(8,128)(2,1)}, bf16[1,2048,96]{1,2,0:T(8,128)(2,1)}) fusion(bf16[288,2048]{1,0:T(8,128)(2,1)} %get-tuple-element.7), kind=kLoop, calls=%fused_computation | loop fusion | bytes 2359296 | tf_op jit(solution)/shard_map/broadcast_in_dim | solution.py:554
  97.7 0.0 copy-done
  97.7 0.6 copy.16
Async XLA Ops:
  95.4 2.3 %copy-start = (bf16[16,128]{1,0:T(8,128)(2,1)S(1)}, bf16[16,128]{1,0:T(8,128)(2,1)}, u32[]{:S(2)}) copy-start(bf16[16,128]{1,0:T(8,128)(2,1)} %get-tuple-element.15) | copy-start | bytes 12292
